TPU v7x, 256 devices: a whole 4x4x8 slice. The times are simulated.
256 devices in a mesh: rep: 4 (over y), fsdp: 64 (over x, z, core).
Axes of the slice: x: 4, y: 4, z: 8, core: 2. Of those that a mesh axis runs over, the one named last changes fastest.
Arguments:
- grad_blocks: bfloat16 [4, 64, 512, 512], P('rep', None, 'fsdp'), may hold values from -6 to 6
- graft_accum: float32 [64, 512, 512], P(None, 'fsdp'), may hold values from 0.1 to 1000000
- left_stats: float32 [128, 512, 512], P('fsdp'), may hold values from -300000 to 300000, as said below
- right_stats: float32 [128, 512, 512], P('fsdp'), may hold values from -300000 to 300000, as said below
- block_slot: int32 [64], replicated, may hold values from 0 to 127, as said below
- vocab_grads: bfloat16 [4, 2, 512, 8192], P('rep', None, 'fsdp'), may hold values from -6 to 6
- vocab_accum: float32 [2, 512, 8192], P(None, 'fsdp'), may hold values from 0.01 to 10
Outputs:
- direction: bfloat16 [64, 512, 512], P(None, 'fsdp')
- graft_accum_new: float32 [64, 512, 512], P(None, 'fsdp')
- left_new: float32 [128, 512, 512], P('fsdp')
- right_new: float32 [128, 512, 512], P('fsdp')
- vocab_accum_new: float32 [2, 512, 8192], P(None, 'fsdp')
- vocab_step: bfloat16 [2, 512, 8192], P(None, 'fsdp')
Inputs may be any that keep to these rules, and one draw needn't show every extreme that they name: Block b's statistics sit in slot block_slot[b]; slot s belongs to fsdp index s // 2; no two blocks name the same slot; every fsdp index owns at most 2 blocks and some index owns exactly 2. `left_stats`: every slot holds a symmetric positive definite matrix. `right_stats`: every slot holds a symmetric positive definite matrix.
All inputs are finite; a program needn't handle non-finite values.
Results may differ from a plain program's by a relative error of at most 0.017.
Values may be sent and summed in bfloat16 or wider, within the bound.
A program may use at most 64 MiB of HBM per device.

v0:
```python
import jax
import jax.numpy as jnp
from jax import lax
from jax.sharding import PartitionSpec as P

ITERS = 6


def as_sent(shard):

    def short(part):
        return part.astype(jnp.bfloat16) if part.dtype == jnp.float32 else part

    return jax.tree.map(short, shard)


def batch_product(left, right):
    return jnp.einsum("sij,sjk->sik", left, right, precision=lax.Precision.HIGHEST)


def batch_root(matrices):
    matrix_order = matrices.shape[-1]
    identity = jnp.eye(matrix_order, dtype=jnp.float32)[None]
    frobenius = jnp.sqrt(jnp.sum(matrices * matrices, axis=(1, 2)))
    scaled = matrices / frobenius[:, None, None]
    result = identity
    for iteration in range(ITERS):
        factor = (5.0 * identity - scaled) * 0.25
        result = factor if iteration == 0 else batch_product(result, factor)
        if iteration + 1 < ITERS:
            square = batch_product(factor, factor)
            fourth = batch_product(square, square)
            scaled = batch_product(fourth, scaled)
    return result


def on_device(
    grad_blocks, graft_accum, left_stats, right_stats, block_slot, vocab_grads, vocab_accum
):
    summed_grad, summed_vocab = (
        lax.psum(grad_blocks[0].astype(jnp.float32).astype(jnp.bfloat16), "rep").astype(
            jnp.float32
        ),
        lax.psum(vocab_grads[0].astype(jnp.float32).astype(jnp.bfloat16), "rep").astype(
            jnp.float32
        ),
    )
    grad_sum = summed_grad.astype(jnp.bfloat16)
    vocab_sum = summed_vocab.astype(jnp.bfloat16)
    vocab_float = vocab_sum.astype(jnp.float32)
    vocab_accum_new = vocab_accum + vocab_float * vocab_float
    vocab_step = (vocab_float / (jnp.sqrt(vocab_accum_new) + 1e-10)).astype(jnp.bfloat16)
    grad_float = grad_sum.astype(jnp.float32)
    graft_accum_new = graft_accum + grad_float * grad_float
    grafted = grad_float / (jnp.sqrt(graft_accum_new) + 1e-10)
    graft_part = jnp.sum(grafted * grafted, axis=(1, 2))
    matrix_order = grad_blocks.shape[-1]
    entries = float(matrix_order * matrix_order)
    slot_count = left_stats.shape[0]
    total_slots = slot_count * lax.axis_size("fsdp")
    onehot = (block_slot[None, :] == jnp.arange(total_slots, dtype=jnp.int32)[:, None]).astype(
        jnp.bfloat16
    )
    outgoing = jnp.einsum(
        "sb,brc->src", onehot, grad_sum, preferred_element_type=jnp.float32
    ).astype(jnp.bfloat16)
    received = lax.all_to_all(outgoing, "fsdp", split_axis=0, concat_axis=1, tiled=True)
    left_new = left_stats + jnp.einsum(
        "sij,skj->sik", received, received, preferred_element_type=jnp.float32
    )
    right_new = right_stats + jnp.einsum(
        "sji,sjk->sik", received, received, preferred_element_type=jnp.float32
    )
    stacked = jnp.concatenate([left_new, right_new], axis=0)
    share_count = stacked.shape[0] // lax.axis_size("rep")
    own_share = lax.dynamic_slice_in_dim(
        stacked, lax.axis_index("rep") * share_count, share_count, 0
    )
    inverse_roots = lax.all_gather(
        batch_root(own_share).astype(jnp.bfloat16), "rep", axis=0, tiled=True
    ).astype(jnp.float32)
    block_float = received.astype(jnp.float32)
    shampoo = batch_product(
        batch_product(inverse_roots[:slot_count], block_float), inverse_roots[slot_count:]
    )
    returned = lax.all_to_all(
        as_sent(shampoo), "fsdp", split_axis=1, concat_axis=0, tiled=True
    ).astype(shampoo.dtype)
    shampoo_rows = jnp.take(returned, block_slot, axis=0)
    shampoo_part = jnp.sum(shampoo_rows * shampoo_rows, axis=(1, 2))
    graft_total, shampoo_total = lax.psum((graft_part, shampoo_part), "fsdp")
    graft_scale = jnp.sqrt(graft_total / entries) / jnp.sqrt(shampoo_total / entries + 1e-06)
    direction = (shampoo_rows * graft_scale[:, None, None]).astype(jnp.bfloat16)
    return (direction, graft_accum_new, left_new, right_new, vocab_accum_new, vocab_step)


def solution(mesh):
    in_specs = (
        P("rep", None, "fsdp", None),
        P(None, "fsdp", None),
        P("fsdp", None, None),
        P("fsdp", None, None),
        P(),
        P("rep", None, "fsdp", None),
        P(None, "fsdp", None),
    )
    out_specs = (
        P(None, "fsdp", None),
        P(None, "fsdp", None),
        P("fsdp", None, None),
        P("fsdp", None, None),
        P(None, "fsdp", None),
        P(None, "fsdp", None),
    )
    return jax.shard_map(
        on_device, mesh=mesh, in_specs=in_specs, out_specs=out_specs, check_vma=False
    )
```

profile of v0, /device:TPU:8, one launch (start us, length us, event | category | flops | bytes accessed | tf_op | source)
XLA Modules:
  0.0 361.6 jit_solution(7396740100654670768)
XLA Ops:
  7.2 2.0 copy.57
  9.2 53.5 %all-reduce.4.cloned.1.call-done = (bf16[64,8,512]{2,0,1:T(8,128)(2,1)}, bf16[2,8,8192]{2,1,0:T(8,128)(2,1)}) async-done(((bf16[64,8,512]{2,0,1:T(8,128)(2,1)}, bf16[2,8,8192]{2,1,0:T(8,128)(2,1)}), (bf16[64,8,512]{2,0,1:T(8,128)(2,1)}, bf16[2,8,8192]{2,1,0:T(8,128)(2,1)})) %all-reduce.4.cloned.1.call-update) | async-done | bytes 786448 | tf_op jit(solution)/shard_map/psum | solution.py:41
  62.8 1.6 convolution_convert_fusion
  64.4 1.5 copy.32
  65.9 10.4 %all-to-all-start = ((bf16[128,8,512]{2,1,0:T(8,128)(2,1)}), bf16[128,8,512]{2,1,0:T(8,128)(2,1)S(1)}, u32[]{:S(2)}, u32[]{:S(2)}) async-start(bf16[128,8,512]{2,1,0:T(8,128)(2,1)} %copy.32), calls=%async_computation | async-start | bytes 2097152 | tf_op jit(solution)/shard_map/all_to_all | solution.py:67
  76.4 0.6 all-gather.3.cloned.1.call-start
  77.0 27.6 %all-to-all-done = bf16[128,8,512]{2,1,0:T(8,128)(2,1)S(1)} async-done(((bf16[128,8,512]{2,1,0:T(8,128)(2,1)}), bf16[128,8,512]{2,1,0:T(8,128)(2,1)S(1)}, u32[]{:S(2)}, u32[]{:S(2)}) %all-to-all-start) | async-done | bytes 1048608 | tf_op jit(solution)/shard_map/all_to_all | solution.py:67
  104.5 2.5 convolution_add_fusion
  107.0 0.8 convolution_add_fusion.1
  107.8 1.3 copy-done.1
  109.1 0.9 multiply_reduce_fusion.1
  110.7 1.5 broadcast_divide_fusion
  112.2 1.9 fusion.12
  114.1 1.8 fusion.102
  116.0 1.8 fusion.8
  117.8 2.0 fusion.10
  119.8 1.9 fusion.31
  121.7 1.8 fusion.103
  123.6 2.0 fusion.104
  125.6 1.9 fusion.27
  127.5 1.9 fusion.29
  129.5 1.8 fusion.105
  131.3 1.8 fusion.106
  133.2 1.9 fusion.23
  135.1 1.9 fusion.25
  137.0 2.1 fusion.107
  139.1 1.8 fusion.108
  140.9 1.9 fusion.19
  142.9 1.9 fusion.21
  144.8 1.8 fusion.109
  146.6 1.9 fusion
  148.5 2.6 convolution_convert_fusion.2
  151.2 29.0 %all-gather.3.cloned.1.call-done = bf16[2048,512]{1,0:T(8,128)(2,1)} async-done(((bf16[512,512]{1,0:T(8,128)(2,1)}), bf16[2048,512]{1,0:T(8,128)(2,1)}) %all-gather.3.cloned.1.call-update) | async-done | bytes 2097168 | tf_op jit(solution)/shard_map/all_gather | solution.py:79
  180.2 1.7 fusion.101
  181.9 0.7 fusion.14
  182.6 2.1 convolution_convert_fusion.1
  184.7 2.0 copy.35
  186.8 10.4 %all-to-all-start.1 = ((bf16[2,512,512]{2,0,1:T(2,128)(2,1)}), bf16[2,512,512]{2,0,1:T(2,128)(2,1)S(1)}, u32[]{:S(2)}, u32[]{:S(2)}) async-start(bf16[2,512,512]{2,0,1:T(2,128)(2,1)} %copy.35), calls=%async_computation.1 | async-start | bytes 2097152 | tf_op jit(solution)/shard_map/all_to_all | solution.py:86
  197.3 0.9 fusion.18
  198.1 1.6 copy.39
  199.7 1.1 fusion.38
  200.8 24.6 %all-to-all-done.1 = bf16[2,512,512]{2,0,1:T(2,128)(2,1)S(1)} async-done(((bf16[2,512,512]{2,0,1:T(2,128)(2,1)}), bf16[2,512,512]{2,0,1:T(2,128)(2,1)S(1)}, u32[]{:S(2)}, u32[]{:S(2)}) %all-to-all-start.1) | async-done | bytes 1048608 | tf_op jit(solution)/shard_map/all_to_all | solution.py:86
  225.4 0.3 convert_bitcast_fusion
  225.6 0.2 copy.37
  225.9 0.6 gather_fusion
  226.5 1.0 multiply_reduce_fusion
  227.5 126.0 %all-reduce = (f32[64]{0:T(128)S(1)}, f32[64]{0:T(128)S(1)}) all-reduce(f32[64]{0:T(128)S(1)} %multiply_reduce_fusion, f32[64]{0:T(128)S(1)} %get-tuple-element.36), channel_id=1, replica_groups=mesh['rep'=4,'fsdp'=64] {'fsdp'}, use_global_device_ids=true, to_apply=%region_5.6 | all-reduce | flops 128 | bytes 1024 | tf_op jit(solution)/shard_map/psum | solution.py:91
  353.5 1.0 multiply_convert_fusion
  (22 shorter events, 0.1 us)
Async XLA Ops:
  7.2 55.6 %all-reduce.4.cloned.1.call-start = ((), (), s32[]{:S(2)}) async-start(), calls=%async_computation.3 | async-start | bytes 1572864 | tf_op jit(solution)/shard_map/psum | solution.py:41
  65.9 38.6 %all-to-all-start = ((bf16[128,8,512]{2,1,0:T(8,128)(2,1)}), bf16[128,8,512]{2,1,0:T(8,128)(2,1)S(1)}, u32[]{:S(2)}, u32[]{:S(2)}) async-start(bf16[128,8,512]{2,1,0:T(8,128)(2,1)} %copy.32), calls=%async_computation | async-start | bytes 2097152 | tf_op jit(solution)/shard_map/all_to_all | solution.py:67
  76.4 103.9 %all-gather.3.cloned.1.call-start = ((), (), s32[]{:S(2)}) async-start(), calls=%async_computation.2 | async-start | bytes 2621440 | tf_op jit(solution)/shard_map/all_gather | solution.py:79
  104.5 2.5 copy-start.2
  107.0 3.7 %copy-start = (f32[2,512,512]{2,1,0:T(8,128)}, f32[2,512,512]{2,1,0:T(8,128)S(1)}, u32[]{:S(2)}) copy-start(f32[2,512,512]{2,1,0:T(8,128)S(1)} %convolution_add_fusion) | copy-start | bytes 6291460
  107.8 1.3 copy-start.1
  148.5 2.7 copy-start.7
  184.7 12.5 %copy-start.3 = (bf16[64,8,512]{2,0,1:T(8,128)(2,1)S(1)}, bf16[64,8,512]{2,0,1:T(8,128)(2,1)}, u32[]{:S(2)}) copy-start(bf16[64,8,512]{2,0,1:T(8,128)(2,1)} %get-tuple-element.32) | copy-start | bytes 1572868
  184.7 12.5 %copy-start.4 = (f32[64,8,512]{2,1,0:T(8,128)S(1)}, f32[64,8,512]{2,1,0:T(8,128)}, u32[]{:S(2)}) copy-start(f32[64,8,512]{2,1,0:T(8,128)} %param.8) | copy-start | bytes 3145732
  186.8 38.6 %all-to-all-start.1 = ((bf16[2,512,512]{2,0,1:T(2,128)(2,1)}), bf16[2,512,512]{2,0,1:T(2,128)(2,1)S(1)}, u32[]{:S(2)}, u32[]{:S(2)}) async-start(bf16[2,512,512]{2,0,1:T(2,128)(2,1)} %copy.35), calls=%async_computation.1 | async-start | bytes 2097152 | tf_op jit(solution)/shard_map/all_to_all | solution.py:86
  197.2 2.5 copy-start.5
  197.3 2.5 copy-start.6
Sparse Core Ops, SparseCore 0:
  11.0 51.6 all-reduce.3
  151.3 28.9 all-gather.2
where the time goes:
time: 364 us; the launch traced here: 362 us
  waiting for transfers between devices  135 us (37%)
  blocking collectives  126 us (35%)
  matrix products  46.4 us (13%)
  starting transfers between devices  21.5 us (6%)
  between operations  15.4 us (4%)
  local copies, waits for them, and re-layouts  11 us (3%)
  other arithmetic  6.57 us (2%)
    psum x1, blocking collectives, on_device(): graft_total, shampoo_total = lax.psum((graft_part, shampoo_part), 'fsdp')  126 us
    psum x1, waiting for transfers between devices, on_device(): lax.psum(grad_blocks[0].astype(jnp.float32).astype(jnp.bfloat16), 'rep')  53.5 us
    dot_general x22, matrix products, batch_product(): jnp.einsum('sij,sjk->sik', left, right, precision=lax.Precision.HIGHEST)  41.6 us
    all_gather x1, waiting for transfers between devices, on_device(): lax.all_gather(batch_root(own_share).astype(jnp.bfloat16), 'rep', axis=0,...  29 us
    all_to_all x1, waiting for transfers between devices, on_device(): lax.all_to_all(outgoing, 'fsdp', split_axis=0, concat_axis=1, tiled=True)  27.6 us
    all_to_all x1, waiting for transfers between devices, on_device(): lax.all_to_all(as_sent(shampoo), 'fsdp', split_axis=1, concat_axis=0, til...  24.6 us
    all_to_all x1, starting transfers between devices, on_device(): lax.all_to_all(as_sent(shampoo), 'fsdp', split_axis=1, concat_axis=0, til...  10.4 us
    all_to_all x1, starting transfers between devices, on_device(): lax.all_to_all(outgoing, 'fsdp', split_axis=0, concat_axis=1, tiled=True)  10.4 us
  transfers between devices with their start and end apart: 4, of which 4 were waited for; matrix products, arithmetic and copies ran while one was open for 1% of the time, Pallas kernels for 0%

commit v1 on v0

v1 whole, which is shorter than its diff:
```python
import functools

import jax
import jax.numpy as jnp
from jax import lax
from jax.experimental import pallas as pl
from jax.experimental.pallas import tpu as pltpu
from jax.sharding import PartitionSpec as P

ITERS = 6
REP = 4
MESH = pl.DeviceIdType.MESH
F32 = jnp.float32
BF16 = jnp.bfloat16
ANY = pl.BlockSpec(memory_space=pl.ANY)
VMEM = pl.BlockSpec(memory_space=pltpu.VMEM)
SMEM = pl.BlockSpec(memory_space=pltpu.SMEM)


def remote(src, dst, send_sem, recv_sem, device):
    return pltpu.make_async_remote_copy(
        src_ref=src,
        dst_ref=dst,
        send_sem=send_sem,
        recv_sem=recv_sem,
        device_id=device,
        device_id_type=MESH,
    )


def enter(rep, own, shards):
    barrier = pltpu.get_barrier_semaphore()

    @pl.loop(1, shards)
    def _(step):
        other = lax.rem(own + step, shards)
        pl.semaphore_signal(barrier, inc=1, device_id=(rep, other), device_id_type=MESH)

    for step in range(1, REP):
        other = lax.rem(rep + step, REP)
        pl.semaphore_signal(barrier, inc=1, device_id=(other, own), device_id_type=MESH)
    return lambda: pl.semaphore_wait(barrier, shards - 1 + REP - 1)


class RingGather:
    def __init__(self, out, rep, own, send_sems, recv_sems):
        self.out, self.send_sems, self.recv_sems = out, send_sems, recv_sems
        right, left = lax.rem(rep + 1, REP), lax.rem(rep + REP - 1, REP)
        far = lax.rem(rep + 2, REP)
        half = out.shape[1] // 2
        first, second = pl.ds(0, half), pl.ds(half, half)
        to_right, to_left = (right, own), (left, own)
        self.sends = (
            self.copy(out.at[rep], 0, to_right),
            self.copy(out.at[rep], 1, to_left),
            self.copy(out.at[left, first], 2, to_right),
            self.copy(out.at[right, second], 3, to_left),
        )
        self.arrivals = (
            self.copy(out.at[left], 0, to_right),
            self.copy(out.at[right], 1, to_left),
            self.copy(out.at[far, first], 2, to_right),
            self.copy(out.at[far, second], 3, to_left),
        )

    def copy(self, piece, index, device):
        return remote(piece, piece, self.send_sems.at[index], self.recv_sems.at[index], device)

    def start(self):
        self.sends[0].start()
        self.sends[1].start()

    def forward(self):
        self.arrivals[0].wait_recv()
        self.sends[2].start()
        self.arrivals[1].wait_recv()
        self.sends[3].start()

    def finish(self):
        self.arrivals[2].wait_recv()
        self.arrivals[3].wait_recv()
        for send in self.sends:
            send.wait_send()


def exchange(shards, rep, own, source, target, send_sems, recv_sems):
    @pl.loop(1, shards)
    def _(step):
        other = lax.rem(own + step, shards)
        remote(source(other), target(own), send_sems.at[other], recv_sems.at[own], (rep, other)).start()

    def finish():
        @pl.loop(1, shards)
        def _(step):
            other = lax.rem(own + step, shards)
            remote(
                source(other), target(other), send_sems.at[other], recv_sems.at[other], (rep, other)
            ).wait_recv()

        @pl.loop(1, shards)
        def _(step):
            other = lax.rem(own + step, shards)
            remote(
                source(other), target(own), send_sems.at[other], recv_sems.at[own], (rep, other)
            ).wait_send()

    return finish


def gather_kernel(
    shards,
    key_ref,
    grad_ref,
    accum_ref,
    vocab_ref,
    slots_out,
    grad_out,
    vocab_out,
    graft_out,
    grad_own,
    grad_terms,
    grad_sum,
    accum_own,
    vocab_own,
    vocab_terms,
    vocab_sum,
    placement,
    outgoing,
    graft_part,
    graft_parts,
    graft_total,
    local_sems,
    term_sends,
    term_recvs,
    slot_sends,
    slot_recvs,
    part_sends,
    part_recvs,
    ring_sends,
    ring_recvs,
):
    rep, own = lax.axis_index("rep"), lax.axis_index("fsdp")
    blocks, rows, quarter = grad_own.shape
    vocab_quarter = vocab_own.shape[-1]

    def grad_columns(index):
        return pl.ds(pl.multiple_of(index * quarter, 128), quarter)

    def vocab_columns(index):
        return pl.ds(pl.multiple_of(index * vocab_quarter, 128), vocab_quarter)

    loads = (
        pltpu.make_async_copy(grad_ref.at[:, :, grad_columns(rep)], grad_own, local_sems.at[0]),
        pltpu.make_async_copy(accum_ref.at[:, :, grad_columns(rep)], accum_own, local_sems.at[1]),
        pltpu.make_async_copy(vocab_ref.at[:, :, vocab_columns(rep)], vocab_own, local_sems.at[2]),
    )
    for load in loads:
        load.start()
    entered = enter(rep, own, shards)

    total_rows = blocks * rows
    key = jnp.broadcast_to(key_ref[...], (shards * rows, total_rows))
    row = lax.broadcasted_iota(jnp.int32, (shards * rows, total_rows), 0)
    place = (row // rows) * (2 * rows) + lax.rem(row, rows)
    for slot in range(2):
        placement[slot] = jnp.where(key == place + slot * rows, 1.0, 0.0).astype(BF16)

    entered()
    grad_copies, vocab_copies = [], []
    for step in range(1, REP):
        other = lax.rem(rep + step, REP)
        grad_copies.append(
            remote(
                grad_ref.at[:, :, grad_columns(other)],
                grad_terms.at[step - 1],
                term_sends.at[step - 1],
                term_recvs.at[step - 1],
                (other, own),
            )
        )
        vocab_copies.append(
            remote(
                vocab_ref.at[:, :, vocab_columns(other)],
                vocab_terms.at[step - 1],
                term_sends.at[REP + step - 2],
                term_recvs.at[REP + step - 2],
                (other, own),
            )
        )
    for copy in grad_copies:
        copy.start()
    loads[0].wait()
    for copy in grad_copies:
        copy.wait_recv()
    total = grad_own[...].astype(F32)
    for step in range(REP - 1):
        total = total + grad_terms[step].astype(F32)
    rounded = total.astype(BF16)
    grad_sum[...] = rounded
    flat = total.reshape(total_rows, quarter).astype(BF16)
    for slot in range(2):
        placed = jnp.dot(placement[slot], flat, preferred_element_type=F32)
        outgoing[:, :, slot * quarter : (slot + 1) * quarter] = placed.reshape(
            shards, rows, quarter
        ).astype(BF16)
    slots_done = exchange(
        shards,
        rep,
        own,
        lambda other: outgoing.at[other],
        lambda source: slots_out.at[rep, source],
        slot_sends,
        slot_recvs,
    )
    keep = pltpu.make_async_copy(outgoing.at[own], slots_out.at[rep, own], local_sems.at[3])
    keep.start()
    for copy in vocab_copies:
        copy.start()
    keep_sum = pltpu.make_async_copy(grad_sum, grad_out.at[rep], local_sems.at[4])
    keep_sum.start()
    keep_sum.wait()
    grad_ring = RingGather(grad_out, rep, own, ring_sends.at[0], ring_recvs.at[0])
    grad_ring.start()

    loads[1].wait()
    value = flat.astype(F32)
    accum_new = accum_own[...].reshape(total_rows, quarter) + value * value
    grafted = value / (jnp.sqrt(accum_new) + 1e-10)
    slot_count = 2 * shards
    slot = lax.broadcasted_iota(jnp.int32, (slot_count, total_rows), 0)
    mine = jnp.where(jnp.broadcast_to(key_ref[...] // rows, (slot_count, total_rows)) == slot, 1.0, 0.0)
    by_slot = jnp.dot(mine, grafted * grafted, precision=lax.Precision.HIGHEST)
    ones = jnp.ones((8, quarter), F32)
    parts = lax.dot_general(
        ones, by_slot, (((1,), (1,)), ((), ())), precision=lax.Precision.HIGHEST
    )
    graft_part[...] = parts[:1]
    graft_parts[pl.ds(own, 1)] = parts[:1][None]
    parts_done = exchange(
        shards,
        rep,
        own,
        lambda other: graft_part,
        lambda source: graft_parts.at[source],
        part_sends,
        part_recvs,
    )

    loads[2].wait()
    for copy in vocab_copies:
        copy.wait_recv()
    vocab_total = vocab_own[...].astype(F32)
    for step in range(REP - 1):
        vocab_total = vocab_total + vocab_terms[step].astype(F32)
    vocab_sum[...] = vocab_total.astype(BF16)
    keep_vocab = pltpu.make_async_copy(vocab_sum, vocab_out.at[rep], local_sems.at[5])
    keep_vocab.start()
    keep_vocab.wait()
    vocab_ring = RingGather(vocab_out, rep, own, ring_sends.at[1], ring_recvs.at[1])
    vocab_ring.start()
    grad_ring.forward()

    keep.wait()
    slots_done()
    slot_ring = RingGather(slots_out, rep, own, ring_sends.at[2], ring_recvs.at[2])
    slot_ring.start()
    vocab_ring.forward()

    parts_done()
    graft_total[...] = jnp.sum(graft_parts[...], axis=0)
    keep_total = pltpu.make_async_copy(graft_total, graft_out.at[rep], local_sems.at[6])
    keep_total.start()
    total_copies = []
    for step in range(1, REP):
        other = lax.rem(rep + step, REP)
        index = 2 * (REP - 1) + step - 1
        copy = remote(
            graft_total, graft_out.at[rep], term_sends.at[index], term_recvs.at[index], (other, own)
        )
        copy.start()
        source = lax.rem(rep + REP - step, REP)
        arrival = remote(
            graft_total, graft_out.at[source], term_sends.at[index], term_recvs.at[index], (other, own)
        )
        total_copies.append((copy, arrival))

    slot_ring.forward()
    grad_ring.finish()
    vocab_ring.finish()
    slot_ring.finish()
    keep_total.wait()
    for copy, arrival in total_copies:
        arrival.wait_recv()
        copy.wait_send()
    for copy in grad_copies + vocab_copies:
        copy.wait_send()


def gather_grads(key, grads, accum, vocab):
    shards = lax.axis_size("fsdp")
    blocks, rows, order = grads.shape
    quarter = order // REP
    vocab_quarter = vocab.shape[-1] // REP
    vocab_shape = vocab.shape[:2] + (vocab_quarter,)
    dma = pltpu.SemaphoreType.DMA
    return pl.pallas_call(
        functools.partial(gather_kernel, shards),
        out_shape=(
            jax.ShapeDtypeStruct((REP, shards, rows, 2 * quarter), BF16),
            jax.ShapeDtypeStruct((REP, blocks, rows, quarter), BF16),
            jax.ShapeDtypeStruct((REP,) + vocab_shape, BF16),
            jax.ShapeDtypeStruct((REP, 1, 2 * shards), F32),
        ),
        in_specs=[VMEM, ANY, ANY, ANY],
        out_specs=(ANY, ANY, ANY, ANY),
        scratch_shapes=[
            pltpu.VMEM((blocks, rows, quarter), BF16),
            pltpu.VMEM((REP - 1, blocks, rows, quarter), BF16),
            pltpu.VMEM((blocks, rows, quarter), BF16),
            pltpu.VMEM((blocks, rows, quarter), F32),
            pltpu.VMEM(vocab_shape, BF16),
            pltpu.VMEM((REP - 1,) + vocab_shape, BF16),
            pltpu.VMEM(vocab_shape, BF16),
            pltpu.VMEM((2, shards * rows, blocks * rows), BF16),
            pltpu.VMEM((shards, rows, 2 * quarter), BF16),
            pltpu.VMEM((1, 2 * shards), F32),
            pltpu.VMEM((shards, 1, 2 * shards), F32),
            pltpu.VMEM((1, 2 * shards), F32),
            dma((7,)),
            dma((3 * (REP - 1),)),
            dma((3 * (REP - 1),)),
            dma((shards,)),
            dma((shards,)),
            dma((shards,)),
            dma((shards,)),
            dma((3, 4)),
            dma((3, 4)),
        ],
        compiler_params=pltpu.CompilerParams(collective_id=0, has_side_effects=True),
        name="gather_grads",
    )(key, grads, accum, vocab)


def return_kernel(shards, mine_ref, out, local_sem, sends, recvs, ring_sends, ring_recvs):
    rep, own = lax.axis_index("rep"), lax.axis_index("fsdp")
    enter(rep, own, shards)()
    done = exchange(
        shards,
        rep,
        own,
        lambda other: mine_ref.at[other],
        lambda source: out.at[rep, source],
        sends,
        recvs,
    )
    keep = pltpu.make_async_copy(mine_ref.at[own], out.at[rep, own], local_sem)
    keep.start()
    keep.wait()
    done()
    ring = RingGather(out, rep, own, ring_sends, ring_recvs)
    ring.start()
    ring.forward()
    ring.finish()


def return_rows(mine):
    shards = lax.axis_size("fsdp")
    dma = pltpu.SemaphoreType.DMA
    return pl.pallas_call(
        functools.partial(return_kernel, shards),
        out_shape=jax.ShapeDtypeStruct((REP,) + mine.shape, BF16),
        in_specs=[ANY],
        out_specs=ANY,
        scratch_shapes=[dma, dma((shards,)), dma((shards,)), dma((4,)), dma((4,))],
        compiler_params=pltpu.CompilerParams(collective_id=1, has_side_effects=True),
        name="return_rows",
    )(mine)


def product(left, right):
    return jnp.dot(left.astype(BF16), right.astype(BF16), preferred_element_type=F32)


def precondition_kernel(
    where_ref,
    slots_ref,
    graft_ref,
    left_ref,
    right_ref,
    mine_out,
    left_out,
    right_out,
    stats,
    scaled,
    result,
    load_sems,
    store_sems,
):
    rep, own = where_ref[0], where_ref[1]
    pick, half = rep // 2, lax.rem(rep, 2)
    order = stats.shape[-1]
    quarter = order // REP
    loads = []
    for turn in range(2):
        slot = pick if turn == 0 else 1 - pick
        for side, ref in enumerate((left_ref, right_ref)):
            loads.append(pltpu.make_async_copy(ref.at[slot], stats.at[turn, side], load_sems.at[turn, side]))
    for load in loads:
        load.start()

    def gradient(slot):
        columns = pl.ds(pl.multiple_of(slot * quarter, 128), quarter)
        return jnp.concatenate(
            [
                slots_ref[index, :, :, columns].astype(F32).reshape(order, quarter).astype(BF16)
                for index in range(REP)
            ],
            axis=1,
        )

    stores = []

    def update(turn):
        slot = pick if turn == 0 else 1 - pick
        grad = gradient(slot)
        for side, out in enumerate((left_out, right_out)):
            axis = 1 - side
            outer = lax.dot_general(grad, grad, (((axis,), (axis,)), ((), ())), preferred_element_type=F32)
            loads[2 * turn + side].wait()
            stats[turn, side] = stats[turn, side] + outer
            store = pltpu.make_async_copy(stats.at[turn, side], out.at[slot], store_sems.at[turn, side])
            store.start()
            stores.append(store)
        return grad

    grad = update(0)
    row = lax.broadcasted_iota(jnp.int32, (order, order), 0)
    column = lax.broadcasted_iota(jnp.int32, (order, order), 1)
    for side in range(2):
        matrix = stats[0, side]
        start = matrix / jnp.sqrt(jnp.sum(matrix * matrix))
        scaled[side] = start
        result[side] = jnp.where(row == column, 1.25, 0.0) - 0.25 * start

    @pl.loop(1, ITERS)
    def _(iteration):
        for side in range(2):
            value = scaled[side]
            excess = product(value, value) * 0.0625 - 0.625 * value
            change = product(excess, excess) + 3.125 * excess
            value = product(change, value) + 2.44140625 * value
            scaled[side] = value
            root = result[side]
            result[side] = 1.25 * root - 0.25 * product(root, value)

    shampoo = product(product(result[0], grad), result[1])
    entries = float(order * order)
    lane = lax.broadcasted_iota(jnp.int32, (1, graft_ref.shape[-1]), 1)
    graft_total = jnp.sum(jnp.where(lane == 2 * own + pick, jnp.sum(graft_ref[...], axis=0), 0.0))
    graft_mean = jnp.full((1, 1), graft_total / entries, F32)
    shampoo_mean = jnp.full((1, 1), jnp.sum(shampoo * shampoo) / entries, F32)
    scale = jnp.sqrt(graft_mean) / jnp.sqrt(shampoo_mean + 1e-06)
    direction = shampoo * scale
    direction = jnp.where(half == 0, direction[:, : order // 2], direction[:, order // 2 :])
    mine_out[...] = direction.reshape(mine_out.shape).astype(BF16)
    update(1)
    for store in stores:
        store.wait()


def precondition(where, slots, graft, left, right):
    rows = slots.shape[2]
    order = left.shape[-1]
    dma = pltpu.SemaphoreType.DMA
    return pl.pallas_call(
        precondition_kernel,
        out_shape=(
            jax.ShapeDtypeStruct((order // rows, rows, order // 2), BF16),
            jax.ShapeDtypeStruct(left.shape, F32),
            jax.ShapeDtypeStruct(right.shape, F32),
        ),
        in_specs=[SMEM, VMEM, VMEM, ANY, ANY],
        out_specs=(VMEM, ANY, ANY),
        scratch_shapes=[
            pltpu.VMEM((2, 2, order, order), F32),
            pltpu.VMEM((2, order, order), F32),
            pltpu.VMEM((2, order, order), F32),
            dma((2, 2)),
            dma((2, 2)),
        ],
        name="precondition",
    )(where, slots, graft, left, right)


def accumulate_kernel(grad_ref, accum_ref, vocab_ref, vocab_accum_ref, accum_out, vocab_out, step_out):
    grad = grad_ref[0].astype(F32)
    accum_out[...] = accum_ref[...] + grad * grad
    vocab = vocab_ref[0].astype(F32)
    vocab_accum = vocab_accum_ref[...] + vocab * vocab
    vocab_out[...] = vocab_accum
    step_out[...] = (vocab / (jnp.sqrt(vocab_accum) + 1e-10)).astype(BF16)


def accumulate(grads, accum, vocab, vocab_accum):
    def piece(array):
        return pl.BlockSpec((1,) + array.shape[1:], lambda index: (index, 0, 0, 0))

    def columns(array):
        return pl.BlockSpec(
            array.shape[:2] + (array.shape[2] // REP,), lambda index: (0, 0, index)
        )

    return pl.pallas_call(
        accumulate_kernel,
        grid=(REP,),
        out_shape=(
            jax.ShapeDtypeStruct(accum.shape, F32),
            jax.ShapeDtypeStruct(vocab_accum.shape, F32),
            jax.ShapeDtypeStruct(vocab_accum.shape, BF16),
        ),
        in_specs=[piece(grads), columns(accum), piece(vocab), columns(vocab_accum)],
        out_specs=(columns(accum), columns(vocab_accum), columns(vocab_accum)),
        name="accumulate",
    )(grads, accum, vocab, vocab_accum)


def select_kernel(slot_ref, rows_ref, out):
    half = rows_ref.shape[-1]

    @pl.loop(0, out.shape[0])
    def _(block):
        slot = slot_ref[block]
        owner, pick = slot // 2, lax.rem(slot, 2)
        for side in range(2):
            out[block, :, side * half : (side + 1) * half] = rows_ref[2 * pick + side, owner]


def select_rows(block_slot, rows):
    return pl.pallas_call(
        select_kernel,
        out_shape=jax.ShapeDtypeStruct(
            (block_slot.shape[0], rows.shape[2], 2 * rows.shape[3]), BF16
        ),
        in_specs=[SMEM, VMEM],
        out_specs=VMEM,
        name="select_rows",
    )(block_slot, rows)


def on_device(
    grad_blocks, graft_accum, left_stats, right_stats, block_slot, vocab_grads, vocab_accum
):
    rows = grad_blocks.shape[2]
    key = (block_slot[:, None] * rows + jnp.arange(rows, dtype=jnp.int32)[None]).reshape(1, -1)
    where = jnp.stack([lax.axis_index("rep"), lax.axis_index("fsdp")]).astype(jnp.int32)
    slots, grads, vocab, graft = gather_grads(key, grad_blocks[0], graft_accum, vocab_grads[0])
    mine, left_new, right_new = precondition(where, slots, graft, left_stats, right_stats)
    returned = return_rows(mine)
    accum_new, vocab_accum_new, vocab_step = accumulate(grads, graft_accum, vocab, vocab_accum)
    direction = select_rows(block_slot, returned)
    return (direction, accum_new, left_new, right_new, vocab_accum_new, vocab_step)


def solution(mesh):
    in_specs = (
        P("rep", None, "fsdp", None),
        P(None, "fsdp", None),
        P("fsdp", None, None),
        P("fsdp", None, None),
        P(),
        P("rep", None, "fsdp", None),
        P(None, "fsdp", None),
    )
    out_specs = (
        P(None, "fsdp", None),
        P(None, "fsdp", None),
        P("fsdp", None, None),
        P("fsdp", None, None),
        P(None, "fsdp", None),
        P(None, "fsdp", None),
    )
    return jax.shard_map(
        on_device, mesh=mesh, in_specs=in_specs, out_specs=out_specs, check_vma=False
    )
```

time: 364 us -> 107 us (0.29)
  waiting for transfers between devices: 135 us -> 0 us
  blocking collectives: 126 us -> 0 us
  Pallas kernels: 0 us -> 102 us
  matrix products: 46.4 us -> 0 us
  starting transfers between devices: 21.5 us -> 0 us
  between operations: 15.4 us -> 0.66 us
  local copies, waits for them, and re-layouts: 11 us -> 0.68 us
  other arithmetic: 6.57 us -> 1.32 us
    psum x1 -> x0, blocking collectives: 126 us -> none  [on_device(): graft_total, shampoo_total = lax.psum((graft_part, shampoo_part), 'fsdp')]
    pallas_call x0 -> x5, Pallas kernels: none -> 102 us  [the longest x1 45.2 us: gather_grads(): pl.pallas_call(functools.partial(gather_kernel, shards), out_shape=(jax.S...]
    psum x1 -> x0, waiting for transfers between devices: 53.5 us -> none  [on_device(): lax.psum(grad_blocks[0].astype(jnp.float32).astype(jnp.bfloat16), 'rep')]
    all_to_all x2 -> x0, waiting for transfers between devices: 52.1 us -> none  [the longest x1 27.6 us: on_device(): lax.all_to_all(outgoing, 'fsdp', split_axis=0, concat_axis=1, tiled=True)]
    dot_general x25 -> x0, matrix products: 46.4 us -> none  [the longest x22 41.6 us: batch_product(): jnp.einsum('sij,sjk->sik', left, right, precision=lax.Precision.HIGHEST)]
    all_gather x1 -> x0, waiting for transfers between devices: 29 us -> none  [on_device(): lax.all_gather(batch_root(own_share).astype(jnp.bfloat16), 'rep', axis=0,...]
    all_to_all x2 -> x0, starting transfers between devices: 20.9 us -> none  [the longest x1 10.4 us: on_device(): lax.all_to_all(as_sent(shampoo), 'fsdp', split_axis=1, concat_axis=0, til...]
    unnamed x18 -> x0, local copies, waits for them, and re-layouts: 4.93 us -> none
  transfers between devices with their start and end apart: 4 -> 0, of which waited for: 4 -> 0; matrix products, arithmetic and copies ran while one was open for 1% -> 0% of each run, Pallas kernels for 0% -> 0%
where the time goes in v1:
time: 107 us; the launch traced here: 105 us
  Pallas kernels  102 us (95%)
  other arithmetic  1.32 us (1%)
    pallas_call x1, Pallas kernels, gather_grads(): pl.pallas_call(functools.partial(gather_kernel, shards), out_shape=(jax.S...  45.2 us
    pallas_call x1, Pallas kernels, return_rows(): pl.pallas_call(functools.partial(return_kernel, shards), out_shape=jax.Sh...  29.5 us
    pallas_call x1, Pallas kernels, precondition(): pl.pallas_call(precondition_kernel, out_shape=(jax.ShapeDtypeStruct((orde...  20.8 us
    pallas_call x1, Pallas kernels, accumulate(): pl.pallas_call(accumulate_kernel, grid=(REP,), out_shape=(jax.ShapeDtypeS...  3.75 us
    pallas_call x1, Pallas kernels, select_rows(): pl.pallas_call(select_kernel, out_shape=jax.ShapeDtypeStruct((block_slot....  2.84 us

profile of v1, /device:TPU:8, one launch (start us, length us, event | category | flops | bytes accessed | tf_op | source)
XLA Modules:
  0.0 104.8 jit_solution(11680590059274715835)
XLA Ops:
  0.6 0.7 broadcast_multiply_fusion
  1.3 0.1 iota_add_fusion
  1.4 0.7 add.26.key_ref
  2.0 45.2 %gather_grads.1 = (bf16[4,64,8,256]{3,2,1,0:T(8,128)(2,1)}, bf16[4,64,8,128]{3,2,1,0:T(8,128)(2,1)}, bf16[4,2,8,2048]{3,2,1,0:T(8,128)(2,1)}, f32[4,1,128]{2,1,0:T(1,128)}) custom-call(s32[1,512]{1,0:T(1,128)} %add.26.key_ref, bf16[64,8,512]{2,1,0:T(8,128)(2,1)} %bitcast.4, f32[64,8,512]{2,1,0:T(8,128)} %accum_ref.3, bf16[2,8,8192]{2,1,0:T(8,128)(2,1)} %bitcast.5), custom_call_target="tpu_custom_call" | custom-call | tf_op jit(solution)/shard_map/gather_grads/pallas_call | solution.py:306
  47.3 0.6 pad_add_fusion.where_ref
  47.8 20.8 %precondition.1 = (bf16[64,8,256]{2,1,0:T(8,128)(2,1)}, f32[2,512,512]{2,1,0:T(8,128)}, f32[2,512,512]{2,1,0:T(8,128)}) custom-call(s32[2]{0:T(128)} %pad_add_fusion.where_ref, bf16[4,64,8,256]{3,2,1,0:T(8,128)(2,1)} %get-tuple-element.16.slots_ref, f32[4,1,128]{2,1,0:T(1,128)} %get-tuple-element.17.graft_ref, f32[2,512,512]{2,1,0:T(8,128)} %left_ref.1, ...), custom_call_target="tpu_custom_call" | custom-call | tf_op jit(solution)/shard_map/precondition/pallas_call | solution.py:475
  68.7 29.5 %return_rows.1.rows_ref = bf16[4,64,8,256]{3,2,1,0:T(8,128)(2,1)} custom-call(bf16[64,8,256]{2,1,0:T(8,128)(2,1)} %get-tuple-element.18.mine_ref), custom_call_target="tpu_custom_call" | custom-call | tf_op jit(solution)/shard_map/return_rows/pallas_call | solution.py:369
  98.2 2.8 %select_rows.1 = bf16[64,8,512]{2,1,0:T(8,128)(2,1)} custom-call(s32[64]{0:T(128)} %slot_ref.1, bf16[4,64,8,256]{3,2,1,0:T(8,128)(2,1)} %return_rows.1.rows_ref), custom_call_target="tpu_custom_call" | custom-call | tf_op jit(solution)/shard_map/select_rows/pallas_call | solution.py:539
  101.0 3.7 %accumulate.1 = (f32[64,8,512]{2,1,0:T(8,128)}, f32[2,8,8192]{2,1,0:T(8,128)}, bf16[2,8,8192]{2,1,0:T(8,128)(2,1)}) custom-call(bf16[4,64,8,128]{3,2,1,0:T(8,128)(2,1)} %get-tuple-element.19.grad_ref, f32[64,8,512]{2,1,0:T(8,128)} %accum_ref.3, bf16[4,2,8,2048]{3,2,1,0:T(8,128)(2,1)} %get-tuple-element.20.vocab_ref, f32[2,8,8192]{2,1,0:T(8,128)} %vocab_accum_ref.1), custom_call_target="tpu_custom_call" | custom-call | tf_op jit(solution)/shard_map/accumulate/pallas_call | solution.py:513

commit v2 on v0

v2 whole, which is shorter than its diff:
```python
import functools

import jax
import jax.numpy as jnp
from jax import lax
from jax.experimental import pallas as pl
from jax.experimental.pallas import tpu as pltpu
from jax.sharding import PartitionSpec as P

ITERS = 6
REP = 4
GROUPS = 4
TURNS = (2, 1, 3, 0)
MESH = pl.DeviceIdType.MESH
F32 = jnp.float32
BF16 = jnp.bfloat16
ANY = pl.BlockSpec(memory_space=pl.ANY)
HBM = pl.BlockSpec(memory_space=pltpu.HBM)
VMEM = pl.BlockSpec(memory_space=pltpu.VMEM)
SMEM = pl.BlockSpec(memory_space=pltpu.SMEM)


def remote(src, dst, send_sem, recv_sem, device):
    return pltpu.make_async_remote_copy(
        src_ref=src,
        dst_ref=dst,
        send_sem=send_sem,
        recv_sem=recv_sem,
        device_id=device,
        device_id_type=MESH,
    )


def enter(rep, own, shards):
    barrier = pltpu.get_barrier_semaphore()

    @pl.loop(1, shards)
    def _(step):
        other = lax.rem(own + step, shards)
        pl.semaphore_signal(barrier, inc=1, device_id=(rep, other), device_id_type=MESH)

    for step in range(1, REP):
        other = lax.rem(rep + step, REP)
        pl.semaphore_signal(barrier, inc=1, device_id=(other, own), device_id_type=MESH)
    return lambda: pl.semaphore_wait(barrier, shards - 1 + REP - 1)


class RingGather:
    def __init__(self, out, first, count, rep, own, send_sems, recv_sems):
        self.send_sems, self.recv_sems = send_sems, recv_sems
        right, left = lax.rem(rep + 1, REP), lax.rem(rep + REP - 1, REP)
        far = lax.rem(rep + 2, REP)
        half = count // 2
        whole, front, back = pl.ds(first, count), pl.ds(first, half), pl.ds(first + half, half)
        to_right, to_left = (right, own), (left, own)
        self.sends = (
            self.copy(out.at[rep, whole], 0, to_right),
            self.copy(out.at[rep, whole], 1, to_left),
            self.copy(out.at[left, front], 2, to_right),
            self.copy(out.at[right, back], 3, to_left),
        )
        self.arrivals = (
            self.copy(out.at[left, whole], 0, to_right),
            self.copy(out.at[right, whole], 1, to_left),
            self.copy(out.at[far, front], 2, to_right),
            self.copy(out.at[far, back], 3, to_left),
        )

    def copy(self, piece, index, device):
        return remote(piece, piece, self.send_sems.at[index], self.recv_sems.at[index], device)

    def start(self):
        self.sends[0].start()
        self.sends[1].start()

    def forward(self):
        self.arrivals[0].wait_recv()
        self.sends[2].start()
        self.arrivals[1].wait_recv()
        self.sends[3].start()

    def finish(self):
        self.arrivals[2].wait_recv()
        self.arrivals[3].wait_recv()

    def sent(self):
        for send in self.sends:
            send.wait_send()


class Exchange:
    def __init__(self, shards, rep, own, source, target, send_sems, recv_sems):
        self.shards, self.rep, self.own = shards, rep, own
        self.source, self.target = source, target
        self.send_sems, self.recv_sems = send_sems, recv_sems
        self.size = shards // GROUPS

    def each(self, turn, body):
        group = lax.rem(self.own // self.size + turn, GROUPS)

        @pl.loop(1 if turn == 0 else 0, self.size)
        def _(step):
            body(group * self.size + lax.rem(self.own + step, self.size))

        return group * self.size

    def sent(self, other):
        return remote(
            self.source(other),
            self.target(self.own),
            self.send_sems.at[other],
            self.recv_sems.at[self.own],
            (self.rep, other),
        )

    def came(self, other):
        return remote(
            self.source(other),
            self.target(other),
            self.send_sems.at[other],
            self.recv_sems.at[other],
            (self.rep, other),
        )

    def start(self):
        for turn in TURNS:
            self.each(turn, lambda other: self.sent(other).start())

    def arrive(self, turn):
        return self.each(GROUPS - turn if turn else 0, lambda other: self.came(other).wait_recv())

    def finish(self):
        for turn in TURNS:
            self.each(turn, lambda other: self.sent(other).wait_send())


def gather_groups(exchange, out, kept, ring_sends, ring_recvs):
    rings = []
    for index, turn in enumerate(TURNS):
        first = exchange.arrive(turn)
        if turn == 0:
            kept.wait()
        ring = RingGather(
            out, first, exchange.size, exchange.rep, exchange.own, ring_sends.at[index], ring_recvs.at[index]
        )
        ring.start()
        if rings:
            rings[-1].forward()
        rings.append(ring)
    rings[-1].forward()
    for ring in rings:
        ring.finish()

    def sent():
        exchange.finish()
        for ring in rings:
            ring.sent()

    return sent


def product(left, right):
    return jnp.dot(left.astype(BF16), right.astype(BF16), preferred_element_type=F32)


def gradient(slots_ref, slot):
    count, shards, rows, width = slots_ref.shape
    columns = pl.ds(pl.multiple_of(slot * (width // 2), 128), width // 2)
    return jnp.concatenate(
        [
            slots_ref[index, :, :, columns].astype(F32).reshape(shards * rows, width // 2).astype(BF16)
            for index in range(count)
        ],
        axis=1,
    )


def outer(grad, side):
    axis = 1 - side
    return lax.dot_general(grad, grad, (((axis,), (axis,)), ((), ())), preferred_element_type=F32)


def step_kernel(
    shards,
    slot_ref,
    grad_ref,
    accum_ref,
    vocab_ref,
    left_ref,
    right_ref,
    slots_out,
    grad_out,
    vocab_out,
    rows_out,
    grad_own,
    grad_terms,
    grad_relay,
    grad_sum,
    accum_own,
    vocab_own,
    vocab_terms,
    vocab_sum,
    placement,
    outgoing,
    slots,
    graft_part,
    graft_parts,
    graft_totals,
    stats,
    scaled,
    result,
    mine,
    local_sems,
    grad_sends,
    grad_recvs,
    term_sends,
    term_recvs,
    slot_sends,
    slot_recvs,
    part_sends,
    part_recvs,
    row_sends,
    row_recvs,
    slot_ring_sends,
    slot_ring_recvs,
    row_ring_sends,
    row_ring_recvs,
    sum_ring_sends,
    sum_ring_recvs,
):
    rep, own = lax.axis_index("rep"), lax.axis_index("fsdp")
    right, left, far = (lax.rem(rep + step, REP) for step in (1, REP - 1, 2))
    to_right, to_left = (right, own), (left, own)
    pick, half = rep // 2, lax.rem(rep, 2)
    blocks, rows, quarter = grad_own.shape
    vocab_quarter = vocab_own.shape[-1]
    order = stats.shape[-1]

    def grad_columns(index):
        return pl.ds(pl.multiple_of(index * quarter, 128), quarter)

    def vocab_columns(index):
        return pl.ds(pl.multiple_of(index * vocab_quarter, 128), vocab_quarter)

    loads = (
        pltpu.make_async_copy(grad_ref.at[:, :, grad_columns(rep)], grad_own, local_sems.at[0]),
        pltpu.make_async_copy(accum_ref.at[:, :, grad_columns(rep)], accum_own, local_sems.at[1]),
        pltpu.make_async_copy(vocab_ref.at[:, :, vocab_columns(rep)], vocab_own, local_sems.at[2]),
        pltpu.make_async_copy(left_ref.at[pick], stats.at[0], local_sems.at[3]),
        pltpu.make_async_copy(right_ref.at[pick], stats.at[1], local_sems.at[4]),
    )
    entered = enter(rep, own, shards)
    for load in loads:
        load.start()

    total_rows = blocks * rows
    spread = jnp.where(
        lax.broadcasted_iota(jnp.int32, (blocks, total_rows), 0)
        == lax.broadcasted_iota(jnp.int32, (blocks, total_rows), 1) // rows,
        1.0,
        0.0,
    )
    slot_of = jnp.broadcast_to(slot_ref[...], (8, blocks)).astype(F32)
    slot_of = product(slot_of, spread)[:1].astype(jnp.int32)
    key = slot_of * rows + lax.rem(lax.broadcasted_iota(jnp.int32, (1, total_rows), 1), rows)
    key = jnp.broadcast_to(key, (shards * rows, total_rows))
    row = lax.broadcasted_iota(jnp.int32, (shards * rows, total_rows), 0)
    place = (row // rows) * (2 * rows) + lax.rem(row, rows)
    for slot in range(2):
        placement[slot] = jnp.where(key == place + slot * rows, 1.0, 0.0).astype(BF16)

    entered()
    front, back = pl.ds(0, blocks // 2), pl.ds(blocks // 2, blocks // 2)
    grad_pairs = (
        (grad_ref.at[front, :, grad_columns(far)], grad_relay.at[0], to_right),
        (grad_ref.at[back, :, grad_columns(far)], grad_relay.at[1], to_left),
        (grad_ref.at[:, :, grad_columns(right)], grad_terms.at[0], to_right),
        (grad_ref.at[:, :, grad_columns(left)], grad_terms.at[1], to_left),
        (grad_relay.at[0], grad_terms.at[2, front], to_right),
        (grad_relay.at[1], grad_terms.at[2, back], to_left),
    )
    grad_copies = [
        remote(source, target, grad_sends.at[index], grad_recvs.at[index], device)
        for index, (source, target, device) in enumerate(grad_pairs)
    ]
    for copy in grad_copies[:4]:
        copy.start()
    vocab_copies = []
    for step in range(1, REP):
        other = lax.rem(rep + step, REP)
        vocab_copies.append(
            remote(
                vocab_ref.at[:, :, vocab_columns(other)],
                vocab_terms.at[step - 1],
                term_sends.at[step - 1],
                term_recvs.at[step - 1],
                (other, own),
            )
        )
    for index in range(2):
        grad_copies[index].wait_recv()
        grad_copies[4 + index].start()
    loads[0].wait()
    for copy in grad_copies[2:]:
        copy.wait_recv()
    total = grad_own[...].astype(F32)
    for step in range(REP - 1):
        total = total + grad_terms[step].astype(F32)
    flat = total.reshape(total_rows, quarter).astype(BF16)
    for slot in range(2):
        placed = jnp.dot(placement[slot], flat, preferred_element_type=F32)
        outgoing[:, :, slot * quarter : (slot + 1) * quarter] = placed.reshape(
            shards, rows, quarter
        ).astype(BF16)
    slot_exchange = Exchange(
        shards,
        rep,
        own,
        lambda other: outgoing.at[other],
        lambda source: slots.at[rep, source],
        slot_sends,
        slot_recvs,
    )
    slot_exchange.start()
    keep = pltpu.make_async_copy(outgoing.at[own], slots.at[rep, own], local_sems.at[5])
    keep.start()
    for copy in vocab_copies:
        copy.start()
    grad_sum[...] = total.astype(BF16)
    keep_sum = pltpu.make_async_copy(grad_sum, grad_out.at[rep], local_sems.at[6])
    keep_sum.start()

    loads[1].wait()
    value = flat.astype(F32)
    accum_new = accum_own[...].reshape(total_rows, quarter) + value * value
    grafted = value / (jnp.sqrt(accum_new) + 1e-10)
    slot_count = 2 * shards
    slot = lax.broadcasted_iota(jnp.int32, (slot_count, total_rows), 0)
    chosen = jnp.where(jnp.broadcast_to(slot_of, (slot_count, total_rows)) == slot, 1.0, 0.0)
    by_slot = jnp.dot(chosen, grafted * grafted, precision=lax.Precision.HIGHEST)
    ones = jnp.ones((8, quarter), F32)
    parts = lax.dot_general(
        ones, by_slot, (((1,), (1,)), ((), ())), precision=lax.Precision.HIGHEST
    )
    graft_part[...] = parts[:1]
    graft_parts[pl.ds(own, 1)] = parts[:1][None]
    part_exchange = Exchange(
        shards,
        rep,
        own,
        lambda other: graft_part,
        lambda source: graft_parts.at[source],
        part_sends,
        part_recvs,
    )
    part_exchange.start()

    slots_sent = gather_groups(slot_exchange, slots, keep, slot_ring_sends, slot_ring_recvs)
    keep_slots = pltpu.make_async_copy(slots, slots_out, local_sems.at[7])
    keep_slots.start()

    keep_sum.wait()
    grad_ring = RingGather(grad_out, 0, blocks, rep, own, sum_ring_sends.at[0], sum_ring_recvs.at[0])
    grad_ring.start()
    loads[2].wait()
    for copy in vocab_copies:
        copy.wait_recv()
    vocab_total = vocab_own[...].astype(F32)
    for step in range(REP - 1):
        vocab_total = vocab_total + vocab_terms[step].astype(F32)
    vocab_sum[...] = vocab_total.astype(BF16)
    keep_vocab = pltpu.make_async_copy(vocab_sum, vocab_out.at[rep], local_sems.at[8])
    keep_vocab.start()

    for turn in TURNS:
        part_exchange.arrive(turn)
    graft_totals[pl.ds(rep, 1)] = jnp.sum(graft_parts[...], axis=0)[None]
    total_copies = []
    for step in range(1, REP):
        other, source = lax.rem(rep + step, REP), lax.rem(rep + REP - step, REP)
        index = REP - 1 + step - 1
        pieces = [graft_totals.at[pl.ds(place, 1)] for place in (rep, source)]
        total_copies.append(
            [remote(piece, piece, term_sends.at[index], term_recvs.at[index], (other, own)) for piece in pieces]
        )
        total_copies[-1][0].start()

    grad = gradient(slots, pick)
    row = lax.broadcasted_iota(jnp.int32, (order, order), 0)
    column = lax.broadcasted_iota(jnp.int32, (order, order), 1)
    for side in range(2):
        loads[3 + side].wait()
        matrix = stats[side] + outer(grad, side)
        start = matrix / jnp.sqrt(jnp.sum(matrix * matrix))
        scaled[side] = start
        result[side] = jnp.where(row == column, 1.25, 0.0) - 0.25 * start
    keep_vocab.wait()
    vocab_ring = RingGather(
        vocab_out, 0, vocab_own.shape[0], rep, own, sum_ring_sends.at[1], sum_ring_recvs.at[1]
    )
    vocab_ring.start()

    @pl.loop(1, ITERS)
    def _(iteration):
        for side in range(2):
            value = scaled[side]
            excess = product(value, value) * 0.0625 - 0.625 * value
            change = product(excess, excess) + 3.125 * excess
            value = product(change, value) + 2.44140625 * value
            scaled[side] = value
            root = result[side]
            result[side] = 1.25 * root - 0.25 * product(root, value)

        @pl.when(iteration == 2)
        def _():
            grad_ring.forward()
            vocab_ring.forward()

    shampoo = product(product(result[0], grad), result[1])
    for copy, arrival in total_copies:
        arrival.wait_recv()
    entries = float(order * order)
    lane = lax.broadcasted_iota(jnp.int32, (1, slot_count), 1)
    graft_total = jnp.sum(jnp.where(lane == 2 * own + pick, jnp.sum(graft_totals[...], axis=0), 0.0))
    graft_mean = jnp.full((1, 1), graft_total / entries, F32)
    shampoo_mean = jnp.full((1, 1), jnp.sum(shampoo * shampoo) / entries, F32)
    scale = jnp.sqrt(graft_mean) / jnp.sqrt(shampoo_mean + 1e-06)
    direction = shampoo * scale
    direction = jnp.where(half == 0, direction[:, : order // 2], direction[:, order // 2 :])
    mine[...] = direction.reshape(mine.shape).astype(BF16)
    row_exchange = Exchange(
        shards,
        rep,
        own,
        lambda other: mine.at[other],
        lambda source: rows_out.at[rep, source],
        row_sends,
        row_recvs,
    )
    row_exchange.start()
    keep_rows = pltpu.make_async_copy(mine.at[own], rows_out.at[rep, own], local_sems.at[9])
    keep_rows.start()
    grad_ring.finish()
    vocab_ring.finish()
    rows_sent = gather_groups(row_exchange, rows_out, keep_rows, row_ring_sends, row_ring_recvs)

    keep_slots.wait()
    for copy in grad_copies + vocab_copies:
        copy.wait_send()
    for copy, arrival in total_copies:
        copy.wait_send()
    part_exchange.finish()
    grad_ring.sent()
    vocab_ring.sent()
    slots_sent()
    rows_sent()


def shampoo_step(block_slot, grads, accum, vocab, left, right):
    shards = lax.axis_size("fsdp")
    blocks, rows, order = grads.shape
    quarter = order // REP
    vocab_shape = vocab.shape[:2] + (vocab.shape[-1] // REP,)
    row_shape = (REP, shards, rows, order // 2)
    dma = pltpu.SemaphoreType.DMA
    return pl.pallas_call(
        functools.partial(step_kernel, shards),
        out_shape=(
            jax.ShapeDtypeStruct(row_shape, BF16),
            jax.ShapeDtypeStruct((REP, blocks, rows, quarter), BF16),
            jax.ShapeDtypeStruct((REP,) + vocab_shape, BF16),
            jax.ShapeDtypeStruct(row_shape, BF16),
        ),
        in_specs=[VMEM, HBM, HBM, HBM, HBM, HBM],
        out_specs=(ANY, ANY, ANY, ANY),
        scratch_shapes=[
            pltpu.VMEM((blocks, rows, quarter), BF16),
            pltpu.VMEM((REP - 1, blocks, rows, quarter), BF16),
            pltpu.VMEM((2, blocks // 2, rows, quarter), BF16),
            pltpu.VMEM((blocks, rows, quarter), BF16),
            pltpu.VMEM((blocks, rows, quarter), F32),
            pltpu.VMEM(vocab_shape, BF16),
            pltpu.VMEM((REP - 1,) + vocab_shape, BF16),
            pltpu.VMEM(vocab_shape, BF16),
            pltpu.VMEM((2, shards * rows, blocks * rows), BF16),
            pltpu.VMEM(row_shape[1:], BF16),
            pltpu.VMEM(row_shape, BF16),
            pltpu.VMEM((1, 2 * shards), F32),
            pltpu.VMEM((shards, 1, 2 * shards), F32),
            pltpu.VMEM((REP, 1, 2 * shards), F32),
            pltpu.VMEM((2, order, order), F32),
            pltpu.VMEM((2, order, order), F32),
            pltpu.VMEM((2, order, order), F32),
            pltpu.VMEM(row_shape[1:], BF16),
            dma((10,)),
            dma((6,)),
            dma((6,)),
            dma((2 * (REP - 1),)),
            dma((2 * (REP - 1),)),
            dma((shards,)),
            dma((shards,)),
            dma((shards,)),
            dma((shards,)),
            dma((shards,)),
            dma((shards,)),
            dma((GROUPS, 4)),
            dma((GROUPS, 4)),
            dma((GROUPS, 4)),
            dma((GROUPS, 4)),
            dma((2, 4)),
            dma((2, 4)),
        ],
        compiler_params=pltpu.CompilerParams(
            collective_id=0, has_side_effects=True, vmem_limit_bytes=30 * 1024 * 1024
        ),
        name="shampoo_step",
    )(
        block_slot.reshape(1, -1),
        *(pltpu.with_memory_space_constraint(array, pltpu.HBM) for array in (grads, accum, vocab, left, right)),
    )


def finish_kernel(
    slot_ref,
    slots_ref,
    grad_ref,
    vocab_ref,
    rows_ref,
    accum_ref,
    left_ref,
    right_ref,
    vocab_accum_ref,
    direction_out,
    accum_out,
    left_out,
    right_out,
    vocab_out,
    step_out,
):
    half = rows_ref.shape[-1]
    for slot in range(2):
        grad = gradient(slots_ref, slot)
        for side, (ref, out) in enumerate(((left_ref, left_out), (right_ref, right_out))):
            out[slot] = ref[slot] + outer(grad, side)
    for index in range(REP):
        quarter, vocab_quarter = grad_ref.shape[-1], vocab_ref.shape[-1]
        columns = slice(index * quarter, (index + 1) * quarter)
        grad = grad_ref[index].astype(F32)
        accum_out[:, :, columns] = accum_ref[:, :, columns] + grad * grad
        columns = slice(index * vocab_quarter, (index + 1) * vocab_quarter)
        vocab = vocab_ref[index].astype(F32)
        vocab_accum = vocab_accum_ref[:, :, columns] + vocab * vocab
        vocab_out[:, :, columns] = vocab_accum
        step_out[:, :, columns] = (vocab / (jnp.sqrt(vocab_accum) + 1e-10)).astype(BF16)

    @pl.loop(0, direction_out.shape[0])
    def _(block):
        slot = slot_ref[block]
        owner, pick = slot // 2, lax.rem(slot, 2)
        for side in range(2):
            direction_out[block, :, side * half : (side + 1) * half] = rows_ref[2 * pick + side, owner]


def finish(block_slot, slots, grads, vocab, rows, accum, left, right, vocab_accum):
    direction = (block_slot.shape[0], rows.shape[2], 2 * rows.shape[3])
    return pl.pallas_call(
        finish_kernel,
        out_shape=(
            jax.ShapeDtypeStruct(direction, BF16),
            jax.ShapeDtypeStruct(accum.shape, F32),
            jax.ShapeDtypeStruct(left.shape, F32),
            jax.ShapeDtypeStruct(right.shape, F32),
            jax.ShapeDtypeStruct(vocab_accum.shape, F32),
            jax.ShapeDtypeStruct(vocab_accum.shape, BF16),
        ),
        in_specs=[SMEM] + [VMEM] * 8,
        out_specs=(VMEM,) * 6,
        compiler_params=pltpu.CompilerParams(vmem_limit_bytes=30 * 1024 * 1024),
        name="finish",
    )(block_slot, slots, grads, vocab, rows, accum, left, right, vocab_accum)


def on_device(
    grad_blocks, graft_accum, left_stats, right_stats, block_slot, vocab_grads, vocab_accum
):
    slots, grads, vocab, rows = shampoo_step(
        block_slot, grad_blocks[0], graft_accum, vocab_grads[0], left_stats, right_stats
    )
    return finish(
        block_slot, slots, grads, vocab, rows, graft_accum, left_stats, right_stats, vocab_accum
    )


def solution(mesh):
    in_specs = (
        P("rep", None, "fsdp", None),
        P(None, "fsdp", None),
        P("fsdp", None, None),
        P("fsdp", None, None),
        P(),
        P("rep", None, "fsdp", None),
        P(None, "fsdp", None),
    )
    out_specs = (
        P(None, "fsdp", None),
        P(None, "fsdp", None),
        P("fsdp", None, None),
        P("fsdp", None, None),
        P(None, "fsdp", None),
        P(None, "fsdp", None),
    )
    return jax.shard_map(
        on_device, mesh=mesh, in_specs=in_specs, out_specs=out_specs, check_vma=False
    )
```

time: 364 us -> 92.2 us (0.25)
  waiting for transfers between devices: 135 us -> 0 us
  blocking collectives: 126 us -> 0 us
  Pallas kernels: 0 us -> 90.8 us
  matrix products: 46.4 us -> 0 us
  starting transfers between devices: 21.5 us -> 0 us
  between operations: 15.4 us -> 0.69 us
  local copies, waits for them, and re-layouts: 11 us -> 0.66 us
  other arithmetic: 6.57 us -> 0 us
    psum x1 -> x0, blocking collectives: 126 us -> none  [on_device(): graft_total, shampoo_total = lax.psum((graft_part, shampoo_part), 'fsdp')]
    pallas_call x0 -> x2, Pallas kernels: none -> 90.8 us  [the longest x1 84.9 us: shampoo_step(): pl.pallas_call(functools.partial(step_kernel, shards), out_shape=(jax.Sha...]
    psum x1 -> x0, waiting for transfers between devices: 53.5 us -> none  [on_device(): lax.psum(grad_blocks[0].astype(jnp.float32).astype(jnp.bfloat16), 'rep')]
    all_to_all x2 -> x0, waiting for transfers between devices: 52.1 us -> none  [the longest x1 27.6 us: on_device(): lax.all_to_all(outgoing, 'fsdp', split_axis=0, concat_axis=1, tiled=True)]
    dot_general x25 -> x0, matrix products: 46.4 us -> none  [the longest x22 41.6 us: batch_product(): jnp.einsum('sij,sjk->sik', left, right, precision=lax.Precision.HIGHEST)]
    all_gather x1 -> x0, waiting for transfers between devices: 29 us -> none  [on_device(): lax.all_gather(batch_root(own_share).astype(jnp.bfloat16), 'rep', axis=0,...]
    all_to_all x2 -> x0, starting transfers between devices: 20.9 us -> none  [the longest x1 10.4 us: on_device(): lax.all_to_all(as_sent(shampoo), 'fsdp', split_axis=1, concat_axis=0, til...]
    unnamed x18 -> x10, local copies, waits for them, and re-layouts: 4.93 us -> 0.66 us
  transfers between devices with their start and end apart: 4 -> 0, of which waited for: 4 -> 0; matrix products, arithmetic and copies ran while one was open for 1% -> 0% of each run, Pallas kernels for 0% -> 0%
where the time goes in v2:
time: 92.2 us; the launch traced here: 92.1 us
  Pallas kernels  90.8 us (98%)
    pallas_call x1, Pallas kernels, shampoo_step(): pl.pallas_call(functools.partial(step_kernel, shards), out_shape=(jax.Sha...  84.9 us
    pallas_call x1, Pallas kernels, finish(): pl.pallas_call(finish_kernel, out_shape=(jax.ShapeDtypeStruct(direction,...  5.88 us

profile of v2, /device:TPU:8, one launch (start us, length us, event | category | flops | bytes accessed | tf_op | source)
XLA Modules:
  0.0 92.1 jit_solution(15408947441743699481)
XLA Ops:
  0.6 0.0 copy-start.4
  0.6 0.6 copy-done.4
  1.3 0.0 copy-start
  1.3 0.0 copy-start.1
  1.3 0.0 copy-start.2
  1.3 0.0 copy-start.3
  1.3 84.9 %shampoo_step.1 = (bf16[4,64,8,256]{3,2,1,0:T(8,128)(2,1)S(1)}, bf16[4,64,8,128]{3,2,1,0:T(8,128)(2,1)S(1)}, bf16[4,2,8,2048]{3,2,1,0:T(8,128)(2,1)S(1)}, bf16[4,64,8,256]{3,2,1,0:T(8,128)(2,1)S(1)}) custom-call(s32[1,64]{1,0:T(1,128)S(1)} %bitcast.3, bf16[64,8,512]{2,1,0:T(8,128)(2,1)} %bitcast.4, f32[64,8,512]{2,1,0:T(8,128)} %accum_ref.3, ...), custom_call_target="tpu_custom_call" | custom-call | tf_op jit(solution)/shard_map/shampoo_step/pallas_call | solution.py:466
  86.2 0.0 copy-done
  86.2 0.0 copy-done.1
  86.2 0.0 copy-done.2
  86.2 0.0 copy-done.3
  86.3 5.9 %finish.1 = (bf16[64,8,512]{2,1,0:T(8,128)(2,1)}, f32[64,8,512]{2,1,0:T(8,128)}, f32[2,512,512]{2,1,0:T(8,128)}, f32[2,512,512]{2,1,0:T(8,128)}, f32[2,8,8192]{2,1,0:T(8,128)}, /*index=5*/bf16[2,8,8192]{2,1,0:T(8,128)(2,1)}) custom-call(s32[64]{0:T(128)S(1)} %copy-done.4, bf16[4,64,8,256]{3,2,1,0:T(8,128)(2,1)S(1)} %get-tuple-element.10.slots_ref, ...), custom_call_target="tpu_custom_call" | custom-call | tf_op jit(solution)/shard_map/finish/pallas_call | solution.py:566
Async XLA Ops:
  0.6 0.7 copy-start.4
  1.3 84.9 %copy-start = (f32[2,512,512]{2,1,0:T(8,128)S(1)}, f32[2,512,512]{2,1,0:T(8,128)}, u32[]{:S(2)}) copy-start(f32[2,512,512]{2,1,0:T(8,128)} %left_ref.3) | copy-start | bytes 6291460
  1.3 84.9 %copy-start.1 = (f32[2,512,512]{2,1,0:T(8,128)S(1)}, f32[2,512,512]{2,1,0:T(8,128)}, u32[]{:S(2)}) copy-start(f32[2,512,512]{2,1,0:T(8,128)} %right_ref.3) | copy-start | bytes 6291460
  1.3 84.9 %copy-start.2 = (f32[64,8,512]{2,1,0:T(8,128)S(1)}, f32[64,8,512]{2,1,0:T(8,128)}, u32[]{:S(2)}) copy-start(f32[64,8,512]{2,1,0:T(8,128)} %accum_ref.3) | copy-start | bytes 3145732
  1.3 84.9 %copy-start.3 = (f32[2,8,8192]{2,1,0:T(8,128)S(1)}, f32[2,8,8192]{2,1,0:T(8,128)}, u32[]{:S(2)}) copy-start(f32[2,8,8192]{2,1,0:T(8,128)} %vocab_accum_ref.1) | copy-start | bytes 1572868

commit v3 on v2

--- a/solution.py
+++ b/solution.py
@@ -10,7 +10,7 @@
 ITERS = 6
 REP = 4
 GROUPS = 4
-TURNS = (2, 1, 3, 0)
+TURNS = (0, 1, 3, 2)
 MESH = pl.DeviceIdType.MESH
 F32 = jnp.float32
 BF16 = jnp.bfloat16
@@ -88,6 +88,68 @@
             send.wait_send()
 
 
+class PairGather:
+    def __init__(self, slots, first, count, rep, own, send_sems, recv_sems):
+        self.send_sems, self.recv_sems = send_sems, recv_sems
+        odd = lax.rem(rep, 2)
+        partner, beside = rep + 1 - 2 * odd, lax.rem(rep + 3 + 2 * odd, REP)
+        far = lax.rem(rep + 2, REP)
+        pick, rows = rep // 2, pl.ds(first, count)
+        other = 1 - pick
+        to_partner, to_beside = (partner, own), (beside, own)
+
+        def copy(slot, index, sem, device):
+            piece = slots.at[slot, index, rows]
+            return remote(piece, piece, send_sems.at[sem], recv_sems.at[sem], device)
+
+        self.sends = (
+            copy(pick, rep, 0, to_partner),
+            copy(other, rep, 1, to_beside),
+            copy(pick, beside, 2, to_partner),
+        )
+        self.arrivals = (
+            copy(pick, partner, 0, to_partner),
+            copy(pick, beside, 1, to_beside),
+            copy(pick, far, 2, to_partner),
+        )
+        self.rest = (
+            copy(other, rep, 3, to_partner),
+            copy(pick, rep, 4, to_beside),
+            copy(pick, partner, 5, to_beside),
+        )
+        self.rest_arrivals = (
+            copy(other, partner, 3, to_partner),
+            copy(other, beside, 4, to_beside),
+            copy(other, far, 5, to_beside),
+        )
+
+    def start(self):
+        self.sends[0].start()
+        self.sends[1].start()
+
+    def forward(self):
+        self.arrivals[1].wait_recv()
+        self.sends[2].start()
+
+    def finish(self):
+        self.arrivals[0].wait_recv()
+        self.arrivals[2].wait_recv()
+
+    def sent(self):
+        for send in self.sends:
+            send.wait_send()
+
+    def start_rest(self):
+        for send in self.rest:
+            send.start()
+
+    def finish_rest(self):
+        for arrival in self.rest_arrivals:
+            arrival.wait_recv()
+        for send in self.rest:
+            send.wait_send()
+
+
 class Exchange:
     def __init__(self, shards, rep, own, source, target, send_sems, recv_sems):
         self.shards, self.rep, self.own = shards, rep, own
@@ -134,13 +196,13 @@
             self.each(turn, lambda other: self.sent(other).wait_send())
 
 
-def gather_groups(exchange, out, kept, ring_sends, ring_recvs):
+def gather_groups(ring_type, exchange, out, kept, ring_sends, ring_recvs):
     rings = []
     for index, turn in enumerate(TURNS):
         first = exchange.arrive(turn)
         if turn == 0:
             kept.wait()
-        ring = RingGather(
+        ring = ring_type(
             out, first, exchange.size, exchange.rep, exchange.own, ring_sends.at[index], ring_recvs.at[index]
         )
         ring.start()
@@ -164,11 +226,10 @@
 
 
 def gradient(slots_ref, slot):
-    count, shards, rows, width = slots_ref.shape
-    columns = pl.ds(pl.multiple_of(slot * (width // 2), 128), width // 2)
+    count, shards, rows, quarter = slots_ref.shape[1:]
     return jnp.concatenate(
         [
-            slots_ref[index, :, :, columns].astype(F32).reshape(shards * rows, width // 2).astype(BF16)
+            slots_ref[slot, index].astype(F32).reshape(shards * rows, quarter).astype(BF16)
             for index in range(count)
         ],
         axis=1,
@@ -192,6 +253,7 @@
     grad_out,
     vocab_out,
     rows_out,
+    slot_own,
     grad_own,
     grad_terms,
     grad_relay,
@@ -227,6 +289,7 @@
     row_ring_recvs,
     sum_ring_sends,
     sum_ring_recvs,
+    slot_rest_sems,
 ):
     rep, own = lax.axis_index("rep"), lax.axis_index("fsdp")
     right, left, far = (lax.rem(rep + step, REP) for step in (1, REP - 1, 2))
@@ -249,6 +312,8 @@
         pltpu.make_async_copy(left_ref.at[pick], stats.at[0], local_sems.at[3]),
         pltpu.make_async_copy(right_ref.at[pick], stats.at[1], local_sems.at[4]),
     )
+    load_slot = pltpu.make_async_copy(slot_ref, slot_own, local_sems.at[10])
+    load_slot.start()
     entered = enter(rep, own, shards)
     for load in loads:
         load.start()
@@ -260,7 +325,8 @@
         1.0,
         0.0,
     )
-    slot_of = jnp.broadcast_to(slot_ref[...], (8, blocks)).astype(F32)
+    load_slot.wait()
+    slot_of = jnp.broadcast_to(slot_own[...], (8, blocks)).astype(F32)
     slot_of = product(slot_of, spread)[:1].astype(jnp.int32)
     key = slot_of * rows + lax.rem(lax.broadcasted_iota(jnp.int32, (1, total_rows), 1), rows)
     key = jnp.broadcast_to(key, (shards * rows, total_rows))
@@ -309,20 +375,18 @@
     flat = total.reshape(total_rows, quarter).astype(BF16)
     for slot in range(2):
         placed = jnp.dot(placement[slot], flat, preferred_element_type=F32)
-        outgoing[:, :, slot * quarter : (slot + 1) * quarter] = placed.reshape(
-            shards, rows, quarter
-        ).astype(BF16)
+        outgoing[:, slot] = placed.reshape(shards, rows, quarter).astype(BF16)
     slot_exchange = Exchange(
         shards,
         rep,
         own,
         lambda other: outgoing.at[other],
-        lambda source: slots.at[rep, source],
+        lambda source: slots.at[:, rep, source],
         slot_sends,
         slot_recvs,
     )
     slot_exchange.start()
-    keep = pltpu.make_async_copy(outgoing.at[own], slots.at[rep, own], local_sems.at[5])
+    keep = pltpu.make_async_copy(outgoing.at[own], slots.at[:, rep, own], local_sems.at[5])
     keep.start()
     for copy in vocab_copies:
         copy.start()
@@ -355,26 +419,16 @@
     )
     part_exchange.start()
 
-    slots_sent = gather_groups(slot_exchange, slots, keep, slot_ring_sends, slot_ring_recvs)
-    keep_slots = pltpu.make_async_copy(slots, slots_out, local_sems.at[7])
-    keep_slots.start()
-
+    slots_sent = gather_groups(PairGather, slot_exchange, slots, keep, slot_ring_sends, slot_ring_recvs)
+    slot_rest = PairGather(slots, 0, shards, rep, own, slot_rest_sems.at[0], slot_rest_sems.at[1])
+    slot_rest.start_rest()
     keep_sum.wait()
     grad_ring = RingGather(grad_out, 0, blocks, rep, own, sum_ring_sends.at[0], sum_ring_recvs.at[0])
     grad_ring.start()
-    loads[2].wait()
-    for copy in vocab_copies:
-        copy.wait_recv()
-    vocab_total = vocab_own[...].astype(F32)
-    for step in range(REP - 1):
-        vocab_total = vocab_total + vocab_terms[step].astype(F32)
-    vocab_sum[...] = vocab_total.astype(BF16)
     keep_vocab = pltpu.make_async_copy(vocab_sum, vocab_out.at[rep], local_sems.at[8])
-    keep_vocab.start()
-
-    for turn in TURNS:
-        part_exchange.arrive(turn)
-    graft_totals[pl.ds(rep, 1)] = jnp.sum(graft_parts[...], axis=0)[None]
+    vocab_ring = RingGather(
+        vocab_out, 0, vocab_own.shape[0], rep, own, sum_ring_sends.at[1], sum_ring_recvs.at[1]
+    )
     total_copies = []
     for step in range(1, REP):
         other, source = lax.rem(rep + step, REP), lax.rem(rep + REP - step, REP)
@@ -383,7 +437,6 @@
         total_copies.append(
             [remote(piece, piece, term_sends.at[index], term_recvs.at[index], (other, own)) for piece in pieces]
         )
-        total_copies[-1][0].start()
 
     grad = gradient(slots, pick)
     row = lax.broadcasted_iota(jnp.int32, (order, order), 0)
@@ -394,11 +447,6 @@
         start = matrix / jnp.sqrt(jnp.sum(matrix * matrix))
         scaled[side] = start
         result[side] = jnp.where(row == column, 1.25, 0.0) - 0.25 * start
-    keep_vocab.wait()
-    vocab_ring = RingGather(
-        vocab_out, 0, vocab_own.shape[0], rep, own, sum_ring_sends.at[1], sum_ring_recvs.at[1]
-    )
-    vocab_ring.start()
 
     @pl.loop(1, ITERS)
     def _(iteration):
@@ -413,8 +461,25 @@
 
         @pl.when(iteration == 2)
         def _():
+            for turn in TURNS:
+                part_exchange.arrive(turn)
+            graft_totals[pl.ds(rep, 1)] = jnp.sum(graft_parts[...], axis=0)[None]
+            for copy, arrival in total_copies:
+                copy.start()
+            loads[2].wait()
+            for copy in vocab_copies:
+                copy.wait_recv()
+            vocab_total = vocab_own[...].astype(F32)
+            for step in range(REP - 1):
+                vocab_total = vocab_total + vocab_terms[step].astype(F32)
+            vocab_sum[...] = vocab_total.astype(BF16)
+            keep_vocab.start()
+
+        @pl.when(iteration == 3)
+        def _():
+            keep_vocab.wait()
+            vocab_ring.start()
             grad_ring.forward()
-            vocab_ring.forward()
 
     shampoo = product(product(result[0], grad), result[1])
     for copy, arrival in total_copies:
@@ -440,10 +505,14 @@
     row_exchange.start()
     keep_rows = pltpu.make_async_copy(mine.at[own], rows_out.at[rep, own], local_sems.at[9])
     keep_rows.start()
+    vocab_ring.forward()
+    slot_rest.finish_rest()
+    keep_slots = pltpu.make_async_copy(slots, slots_out, local_sems.at[7])
+    keep_slots.start()
+    rows_sent = gather_groups(RingGather, row_exchange, rows_out, keep_rows, row_ring_sends, row_ring_recvs)
+
     grad_ring.finish()
     vocab_ring.finish()
-    rows_sent = gather_groups(row_exchange, rows_out, keep_rows, row_ring_sends, row_ring_recvs)
-
     keep_slots.wait()
     for copy in grad_copies + vocab_copies:
         copy.wait_send()
@@ -462,18 +531,20 @@
     quarter = order // REP
     vocab_shape = vocab.shape[:2] + (vocab.shape[-1] // REP,)
     row_shape = (REP, shards, rows, order // 2)
+    slot_shape = (2, REP, shards, rows, quarter)
     dma = pltpu.SemaphoreType.DMA
     return pl.pallas_call(
         functools.partial(step_kernel, shards),
         out_shape=(
-            jax.ShapeDtypeStruct(row_shape, BF16),
+            jax.ShapeDtypeStruct(slot_shape, BF16),
             jax.ShapeDtypeStruct((REP, blocks, rows, quarter), BF16),
             jax.ShapeDtypeStruct((REP,) + vocab_shape, BF16),
             jax.ShapeDtypeStruct(row_shape, BF16),
         ),
-        in_specs=[VMEM, HBM, HBM, HBM, HBM, HBM],
+        in_specs=[HBM] * 6,
         out_specs=(ANY, ANY, ANY, ANY),
         scratch_shapes=[
+            pltpu.VMEM((1, blocks), jnp.int32),
             pltpu.VMEM((blocks, rows, quarter), BF16),
             pltpu.VMEM((REP - 1, blocks, rows, quarter), BF16),
             pltpu.VMEM((2, blocks // 2, rows, quarter), BF16),
@@ -483,8 +554,8 @@
             pltpu.VMEM((REP - 1,) + vocab_shape, BF16),
             pltpu.VMEM(vocab_shape, BF16),
             pltpu.VMEM((2, shards * rows, blocks * rows), BF16),
-            pltpu.VMEM(row_shape[1:], BF16),
-            pltpu.VMEM(row_shape, BF16),
+            pltpu.VMEM((shards, 2, rows, quarter), BF16),
+            pltpu.VMEM(slot_shape, BF16),
             pltpu.VMEM((1, 2 * shards), F32),
             pltpu.VMEM((shards, 1, 2 * shards), F32),
             pltpu.VMEM((REP, 1, 2 * shards), F32),
@@ -492,7 +563,7 @@
             pltpu.VMEM((2, order, order), F32),
             pltpu.VMEM((2, order, order), F32),
             pltpu.VMEM(row_shape[1:], BF16),
-            dma((10,)),
+            dma((11,)),
             dma((6,)),
             dma((6,)),
             dma((2 * (REP - 1),)),
@@ -503,20 +574,23 @@
             dma((shards,)),
             dma((shards,)),
             dma((shards,)),
-            dma((GROUPS, 4)),
-            dma((GROUPS, 4)),
+            dma((GROUPS, 6)),
+            dma((GROUPS, 6)),
             dma((GROUPS, 4)),
             dma((GROUPS, 4)),
             dma((2, 4)),
             dma((2, 4)),
+            dma((2, 6)),
         ],
         compiler_params=pltpu.CompilerParams(
             collective_id=0, has_side_effects=True, vmem_limit_bytes=30 * 1024 * 1024
         ),
         name="shampoo_step",
     )(
-        block_slot.reshape(1, -1),
-        *(pltpu.with_memory_space_constraint(array, pltpu.HBM) for array in (grads, accum, vocab, left, right)),
+        *(
+            pltpu.with_memory_space_constraint(array, pltpu.HBM)
+            for array in (block_slot.reshape(1, -1), grads, accum, vocab, left, right)
+        )
     )
 
 
@@ -536,29 +610,51 @@
     right_out,
     vocab_out,
     step_out,
+    direction,
+    accum,
+    stats,
+    vocab_accum,
+    vocab_step,
+    sems,
 ):
     half = rows_ref.shape[-1]
+    stores = []
+
+    def store(source, target):
+        stores.append(pltpu.make_async_copy(source, target, sems.at[len(stores)]))
+        stores[-1].start()
+
     for slot in range(2):
         grad = gradient(slots_ref, slot)
         for side, (ref, out) in enumerate(((left_ref, left_out), (right_ref, right_out))):
-            out[slot] = ref[slot] + outer(grad, side)
+            stats[side, slot] = ref[slot] + outer(grad, side)
+            store(stats.at[side, slot], out.at[slot])
     for index in range(REP):
-        quarter, vocab_quarter = grad_ref.shape[-1], vocab_ref.shape[-1]
+        quarter = grad_ref.shape[-1]
         columns = slice(index * quarter, (index + 1) * quarter)
         grad = grad_ref[index].astype(F32)
-        accum_out[:, :, columns] = accum_ref[:, :, columns] + grad * grad
-        columns = slice(index * vocab_quarter, (index + 1) * vocab_quarter)
+        accum[:, :, columns] = accum_ref[:, :, columns] + grad * grad
+    store(accum, accum_out)
+    for index in range(REP):
+        quarter = vocab_ref.shape[-1]
+        columns = slice(index * quarter, (index + 1) * quarter)
         vocab = vocab_ref[index].astype(F32)
-        vocab_accum = vocab_accum_ref[:, :, columns] + vocab * vocab
-        vocab_out[:, :, columns] = vocab_accum
-        step_out[:, :, columns] = (vocab / (jnp.sqrt(vocab_accum) + 1e-10)).astype(BF16)
-
-    @pl.loop(0, direction_out.shape[0])
+        value = vocab_accum_ref[:, :, columns] + vocab * vocab
+        vocab_accum[:, :, columns] = value
+        vocab_step[:, :, columns] = (vocab / (jnp.sqrt(value) + 1e-10)).astype(BF16)
+    store(vocab_accum, vocab_out)
+    store(vocab_step, step_out)
+
+    @pl.loop(0, direction.shape[0], unroll=4)
     def _(block):
         slot = slot_ref[block]
         owner, pick = slot // 2, lax.rem(slot, 2)
         for side in range(2):
-            direction_out[block, :, side * half : (side + 1) * half] = rows_ref[2 * pick + side, owner]
+            direction[block, :, side * half : (side + 1) * half] = rows_ref[2 * pick + side, owner]
+
+    store(direction, direction_out)
+    for copy in stores:
+        copy.wait()
 
 
 def finish(block_slot, slots, grads, vocab, rows, accum, left, right, vocab_accum):
@@ -574,7 +670,15 @@
             jax.ShapeDtypeStruct(vocab_accum.shape, BF16),
         ),
         in_specs=[SMEM] + [VMEM] * 8,
-        out_specs=(VMEM,) * 6,
+        out_specs=(HBM,) * 6,
+        scratch_shapes=[
+            pltpu.VMEM(direction, BF16),
+            pltpu.VMEM(accum.shape, F32),
+            pltpu.VMEM((2,) + left.shape, F32),
+            pltpu.VMEM(vocab_accum.shape, F32),
+            pltpu.VMEM(vocab_accum.shape, BF16),
+            pltpu.SemaphoreType.DMA((8,)),
+        ],
         compiler_params=pltpu.CompilerParams(vmem_limit_bytes=30 * 1024 * 1024),
         name="finish",
     )(block_slot, slots, grads, vocab, rows, accum, left, right, vocab_accum)

time: 92.2 us -> 86.1 us (0.934)
  Pallas kernels: 90.8 us -> 85.2 us
    pallas_call x1, Pallas kernels: 84.9 us -> 81.4 us  [shampoo_step(): pl.pallas_call(functools.partial(step_kernel, shards), out_shape=(jax.Sha...]
    pallas_call x1, Pallas kernels: 5.88 us -> 3.83 us  [finish(): pl.pallas_call(finish_kernel, out_shape=(jax.ShapeDtypeStruct(direction,...]
where the time goes in v3:
time: 86.1 us; the launch traced here: 85.9 us
  Pallas kernels  85.2 us (99%)
    pallas_call x1, Pallas kernels, shampoo_step(): pl.pallas_call(functools.partial(step_kernel, shards), out_shape=(jax.Sha...  81.4 us
    pallas_call x1, Pallas kernels, finish(): pl.pallas_call(finish_kernel, out_shape=(jax.ShapeDtypeStruct(direction,...  3.83 us

profile of v3, /device:TPU:8, one launch (start us, length us, event | category | flops | bytes accessed | tf_op | source)
XLA Modules:
  0.0 85.9 jit_solution(6773084512068216270)
XLA Ops:
  0.6 0.0 copy-start
  0.6 0.0 copy-start.1
  0.7 0.0 copy-start.2
  0.7 0.0 copy-start.3
  0.7 0.0 copy-start.4
  0.7 81.4 %shampoo_step.1 = (bf16[2,4,64,8,128]{4,3,2,1,0:T(8,128)(2,1)S(1)}, bf16[4,64,8,128]{3,2,1,0:T(8,128)(2,1)S(1)}, bf16[4,2,8,2048]{3,2,1,0:T(8,128)(2,1)S(1)}, bf16[4,64,8,256]{3,2,1,0:T(8,128)(2,1)S(1)}) custom-call(s32[1,64]{1,0:T(1,128)} %bitcast.3, bf16[64,8,512]{2,1,0:T(8,128)(2,1)} %bitcast.4, f32[64,8,512]{2,1,0:T(8,128)} %accum_ref.3, ...), custom_call_target="tpu_custom_call" | custom-call | tf_op jit(solution)/shard_map/shampoo_step/pallas_call | solution.py:536
  82.0 0.0 copy-done
  82.1 0.0 copy-done.1
  82.1 0.0 copy-done.2
  82.1 0.0 copy-done.3
  82.1 0.0 copy-done.4
  82.1 3.8 %finish.1 = (bf16[64,8,512]{2,1,0:T(8,128)(2,1)}, f32[64,8,512]{2,1,0:T(8,128)}, f32[2,512,512]{2,1,0:T(8,128)}, f32[2,512,512]{2,1,0:T(8,128)}, f32[2,8,8192]{2,1,0:T(8,128)}, /*index=5*/bf16[2,8,8192]{2,1,0:T(8,128)(2,1)}) custom-call(s32[64]{0:T(128)S(1)} %copy-done.4, bf16[2,4,64,8,128]{4,3,2,1,0:T(8,128)(2,1)S(1)} %get-tuple-element.10.slots_ref, ...), custom_call_target="tpu_custom_call" | custom-call | tf_op jit(solution)/shard_map/finish/pallas_call | solution.py:662
Async XLA Ops:
  0.6 81.4 %copy-start = (f32[2,512,512]{2,1,0:T(8,128)S(1)}, f32[2,512,512]{2,1,0:T(8,128)}, u32[]{:S(2)}) copy-start(f32[2,512,512]{2,1,0:T(8,128)} %left_ref.3) | copy-start | bytes 6291460
  0.6 81.4 %copy-start.1 = (f32[2,512,512]{2,1,0:T(8,128)S(1)}, f32[2,512,512]{2,1,0:T(8,128)}, u32[]{:S(2)}) copy-start(f32[2,512,512]{2,1,0:T(8,128)} %right_ref.3) | copy-start | bytes 6291460
  0.7 81.4 %copy-start.2 = (f32[64,8,512]{2,1,0:T(8,128)S(1)}, f32[64,8,512]{2,1,0:T(8,128)}, u32[]{:S(2)}) copy-start(f32[64,8,512]{2,1,0:T(8,128)} %accum_ref.3) | copy-start | bytes 3145732
  0.7 81.4 %copy-start.3 = (f32[2,8,8192]{2,1,0:T(8,128)S(1)}, f32[2,8,8192]{2,1,0:T(8,128)}, u32[]{:S(2)}) copy-start(f32[2,8,8192]{2,1,0:T(8,128)} %vocab_accum_ref.1) | copy-start | bytes 1572868
  0.7 81.4 %copy-start.4 = (s32[64]{0:T(128)S(1)}, s32[64]{0:T(128)}, u32[]{:S(2)}) copy-start(s32[64]{0:T(128)} %slot_ref.1) | copy-start | bytes 772

commit v4 on v3

--- a/solution.py
+++ b/solution.py
@@ -151,49 +151,47 @@
 
 
 class Exchange:
-    def __init__(self, shards, rep, own, source, target, send_sems, recv_sems):
+    def __init__(self, shards, rep, own, source, target, span, send_sem, recv_sems):
         self.shards, self.rep, self.own = shards, rep, own
-        self.source, self.target = source, target
-        self.send_sems, self.recv_sems = send_sems, recv_sems
+        self.source, self.target, self.span = source, target, span
+        self.send_sem, self.recv_sems = send_sem, recv_sems
         self.size = shards // GROUPS
 
-    def each(self, turn, body):
-        group = lax.rem(self.own // self.size + turn, GROUPS)
-
-        @pl.loop(1 if turn == 0 else 0, self.size)
-        def _(step):
-            body(group * self.size + lax.rem(self.own + step, self.size))
-
-        return group * self.size
-
-    def sent(self, other):
-        return remote(
-            self.source(other),
-            self.target(self.own),
-            self.send_sems.at[other],
-            self.recv_sems.at[self.own],
-            (self.rep, other),
-        )
-
-    def came(self, other):
-        return remote(
-            self.source(other),
-            self.target(other),
-            self.send_sems.at[other],
-            self.recv_sems.at[other],
-            (self.rep, other),
-        )
-
     def start(self):
+        size = self.size
         for turn in TURNS:
-            self.each(turn, lambda other: self.sent(other).start())
+            group = lax.rem(self.own // size + turn, GROUPS)
+
+            def send(step):
+                other = group * size + lax.rem(self.own + step, size)
+                remote(
+                    self.source(other),
+                    self.target(self.own),
+                    self.send_sem,
+                    self.recv_sems.at[turn],
+                    (self.rep, other),
+                ).start()
+
+            @pl.loop(0, size // 2 - 1)
+            def _(away):
+                send(size // 2 + away)
+                send(size // 2 - 1 - away)
+
+            send(size - 1)
+            if turn:
+                send(0)
+
+    def whole(self, first, count, turn):
+        span = self.span(first, count)
+        return remote(span, span, self.send_sem, self.recv_sems.at[turn], (self.rep, self.own))
 
     def arrive(self, turn):
-        return self.each(GROUPS - turn if turn else 0, lambda other: self.came(other).wait_recv())
+        first = lax.rem(self.own // self.size + GROUPS - turn, GROUPS) * self.size
+        self.whole(first, self.size if turn else self.size - 1, turn).wait_recv()
+        return first
 
     def finish(self):
-        for turn in TURNS:
-            self.each(turn, lambda other: self.sent(other).wait_send())
+        self.whole(0, self.shards - 1, 0).wait_send()
 
 
 def gather_groups(ring_type, exchange, out, kept, ring_sends, ring_recvs):
@@ -382,6 +380,7 @@
         own,
         lambda other: outgoing.at[other],
         lambda source: slots.at[:, rep, source],
+        lambda first, count: slots.at[:, rep, pl.ds(first, count)],
         slot_sends,
         slot_recvs,
     )
@@ -414,6 +413,7 @@
         own,
         lambda other: graft_part,
         lambda source: graft_parts.at[source],
+        lambda first, count: graft_parts.at[pl.ds(first, count)],
         part_sends,
         part_recvs,
     )
@@ -444,7 +444,7 @@
     for side in range(2):
         loads[3 + side].wait()
         matrix = stats[side] + outer(grad, side)
-        start = matrix / jnp.sqrt(jnp.sum(matrix * matrix))
+        start = matrix * (1.0 / jnp.sqrt(jnp.full((1, 1), jnp.sum(matrix * matrix), F32)))
         scaled[side] = start
         result[side] = jnp.where(row == column, 1.25, 0.0) - 0.25 * start
 
@@ -459,7 +459,7 @@
             root = result[side]
             result[side] = 1.25 * root - 0.25 * product(root, value)
 
-        @pl.when(iteration == 2)
+        @pl.when(iteration == 3)
         def _():
             for turn in TURNS:
                 part_exchange.arrive(turn)
@@ -475,11 +475,10 @@
             vocab_sum[...] = vocab_total.astype(BF16)
             keep_vocab.start()
 
-        @pl.when(iteration == 3)
+        @pl.when(iteration == 4)
         def _():
             keep_vocab.wait()
             vocab_ring.start()
-            grad_ring.forward()
 
     shampoo = product(product(result[0], grad), result[1])
     for copy, arrival in total_copies:
@@ -499,12 +498,14 @@
         own,
         lambda other: mine.at[other],
         lambda source: rows_out.at[rep, source],
+        lambda first, count: rows_out.at[rep, pl.ds(first, count)],
         row_sends,
         row_recvs,
     )
     row_exchange.start()
     keep_rows = pltpu.make_async_copy(mine.at[own], rows_out.at[rep, own], local_sems.at[9])
     keep_rows.start()
+    grad_ring.forward()
     vocab_ring.forward()
     slot_rest.finish_rest()
     keep_slots = pltpu.make_async_copy(slots, slots_out, local_sems.at[7])
@@ -568,12 +569,12 @@
             dma((6,)),
             dma((2 * (REP - 1),)),
             dma((2 * (REP - 1),)),
-            dma((shards,)),
-            dma((shards,)),
-            dma((shards,)),
-            dma((shards,)),
-            dma((shards,)),
-            dma((shards,)),
+            dma,
+            dma((GROUPS,)),
+            dma,
+            dma((GROUPS,)),
+            dma,
+            dma((GROUPS,)),
             dma((GROUPS, 6)),
             dma((GROUPS, 6)),
             dma((GROUPS, 4)),

time: 86.1 us -> 77.9 us (0.905)
  Pallas kernels: 85.2 us -> 77 us
    pallas_call x1, Pallas kernels: 81.4 us -> 73.2 us  [shampoo_step(): pl.pallas_call(functools.partial(step_kernel, shards), out_shape=(jax.Sha...]
where the time goes in v4:
time: 77.9 us; the launch traced here: 77.7 us
  Pallas kernels  77 us (99%)
    pallas_call x1, Pallas kernels, shampoo_step(): pl.pallas_call(functools.partial(step_kernel, shards), out_shape=(jax.Sha...  73.2 us
    pallas_call x1, Pallas kernels, finish(): pl.pallas_call(finish_kernel, out_shape=(jax.ShapeDtypeStruct(direction,...  3.83 us

profile of v4, /device:TPU:8, one launch (start us, length us, event | category | flops | bytes accessed | tf_op | source)
XLA Modules:
  0.0 77.7 jit_solution(9871600432060225421)
XLA Ops:
  0.6 0.0 copy-start
  0.6 0.0 copy-start.1
  0.7 0.0 copy-start.2
  0.7 0.0 copy-start.3
  0.7 0.0 copy-start.4
  0.7 73.2 %shampoo_step.1 = (bf16[2,4,64,8,128]{4,3,2,1,0:T(8,128)(2,1)S(1)}, bf16[4,64,8,128]{3,2,1,0:T(8,128)(2,1)S(1)}, bf16[4,2,8,2048]{3,2,1,0:T(8,128)(2,1)S(1)}, bf16[4,64,8,256]{3,2,1,0:T(8,128)(2,1)S(1)}) custom-call(s32[1,64]{1,0:T(1,128)} %bitcast.3, bf16[64,8,512]{2,1,0:T(8,128)(2,1)} %bitcast.4, f32[64,8,512]{2,1,0:T(8,128)} %accum_ref.3, ...), custom_call_target="tpu_custom_call" | custom-call | tf_op jit(solution)/shard_map/shampoo_step/pallas_call | solution.py:537
  73.8 0.0 copy-done
  73.9 0.0 copy-done.1
  73.9 0.0 copy-done.2
  73.9 0.0 copy-done.3
  73.9 0.0 copy-done.4
  73.9 3.8 %finish.1 = (bf16[64,8,512]{2,1,0:T(8,128)(2,1)}, f32[64,8,512]{2,1,0:T(8,128)}, f32[2,512,512]{2,1,0:T(8,128)}, f32[2,512,512]{2,1,0:T(8,128)}, f32[2,8,8192]{2,1,0:T(8,128)}, /*index=5*/bf16[2,8,8192]{2,1,0:T(8,128)(2,1)}) custom-call(s32[64]{0:T(128)S(1)} %copy-done.4, bf16[2,4,64,8,128]{4,3,2,1,0:T(8,128)(2,1)S(1)} %get-tuple-element.10.slots_ref, ...), custom_call_target="tpu_custom_call" | custom-call | tf_op jit(solution)/shard_map/finish/pallas_call | solution.py:663
Async XLA Ops:
  0.6 73.2 %copy-start = (f32[2,512,512]{2,1,0:T(8,128)S(1)}, f32[2,512,512]{2,1,0:T(8,128)}, u32[]{:S(2)}) copy-start(f32[2,512,512]{2,1,0:T(8,128)} %left_ref.3) | copy-start | bytes 6291460
  0.6 73.2 %copy-start.1 = (f32[2,512,512]{2,1,0:T(8,128)S(1)}, f32[2,512,512]{2,1,0:T(8,128)}, u32[]{:S(2)}) copy-start(f32[2,512,512]{2,1,0:T(8,128)} %right_ref.3) | copy-start | bytes 6291460
  0.7 73.2 %copy-start.2 = (f32[64,8,512]{2,1,0:T(8,128)S(1)}, f32[64,8,512]{2,1,0:T(8,128)}, u32[]{:S(2)}) copy-start(f32[64,8,512]{2,1,0:T(8,128)} %accum_ref.3) | copy-start | bytes 3145732
  0.7 73.2 %copy-start.3 = (f32[2,8,8192]{2,1,0:T(8,128)S(1)}, f32[2,8,8192]{2,1,0:T(8,128)}, u32[]{:S(2)}) copy-start(f32[2,8,8192]{2,1,0:T(8,128)} %vocab_accum_ref.1) | copy-start | bytes 1572868
  0.7 73.2 %copy-start.4 = (s32[64]{0:T(128)S(1)}, s32[64]{0:T(128)}, u32[]{:S(2)}) copy-start(s32[64]{0:T(128)} %slot_ref.1) | copy-start | bytes 772

commit v5 on v4

--- a/solution.py
+++ b/solution.py
@@ -34,10 +34,14 @@
 def enter(rep, own, shards):
     barrier = pltpu.get_barrier_semaphore()
 
-    @pl.loop(1, shards)
-    def _(step):
-        other = lax.rem(own + step, shards)
-        pl.semaphore_signal(barrier, inc=1, device_id=(rep, other), device_id_type=MESH)
+    size = shards // GROUPS
+    for turn in (2, 1, 3, 0):
+        group = lax.rem(own // size + turn, GROUPS)
+
+        @pl.loop(1 if turn == 0 else 0, size)
+        def _(step):
+            other = group * size + lax.rem(own + step, size)
+            pl.semaphore_signal(barrier, inc=1, device_id=(rep, other), device_id_type=MESH)
 
     for step in range(1, REP):
         other = lax.rem(rep + step, REP)
@@ -220,7 +224,34 @@
 
 
 def product(left, right):
-    return jnp.dot(left.astype(BF16), right.astype(BF16), preferred_element_type=F32)
+    return jnp.dot(left, right, preferred_element_type=F32)
+
+
+def symmetric_product(left, right, side):
+    half = left.shape[-1] // 2
+    return product(left[side, :half], right[side, :, :half]), product(left[side], right[side, :, half:])
+
+
+def parts_of(matrix, side):
+    half = matrix.shape[-1] // 2
+    return matrix[side, :half, :half], matrix[side, :, half:]
+
+
+def put_parts(matrix, side, parts):
+    half = matrix.shape[-1] // 2
+    matrix[side, :half, :half] = parts[0]
+    matrix[side, :, half:] = parts[1]
+
+
+def put_operand(matrix, side, parts):
+    half = matrix.shape[-1] // 2
+    corner, right = (part.astype(BF16) for part in parts)
+    put_parts(matrix, side, (corner, right))
+    matrix[side, half:, :half] = right[:half].T
+
+
+def combine(parts, factor, others, other_factor):
+    return tuple(part * factor + other * other_factor for part, other in zip(parts, others))
 
 
 def gradient(slots_ref, slot):
@@ -269,6 +300,10 @@
     stats,
     scaled,
     result,
+    scaled_operand,
+    excess_operand,
+    change_operand,
+    result_operand,
     mine,
     local_sems,
     grad_sends,
@@ -325,7 +360,7 @@
     )
     load_slot.wait()
     slot_of = jnp.broadcast_to(slot_own[...], (8, blocks)).astype(F32)
-    slot_of = product(slot_of, spread)[:1].astype(jnp.int32)
+    slot_of = product(slot_of.astype(BF16), spread.astype(BF16))[:1].astype(jnp.int32)
     key = slot_of * rows + lax.rem(lax.broadcasted_iota(jnp.int32, (1, total_rows), 1), rows)
     key = jnp.broadcast_to(key, (shards * rows, total_rows))
     row = lax.broadcasted_iota(jnp.int32, (shards * rows, total_rows), 0)
@@ -439,25 +474,56 @@
         )
 
     grad = gradient(slots, pick)
+    middle = order // 2
     row = lax.broadcasted_iota(jnp.int32, (order, order), 0)
     column = lax.broadcasted_iota(jnp.int32, (order, order), 1)
+    identity = jnp.where(row == column, 1.25, 0.0)
+    identity = (identity[:middle, :middle], identity[:, middle:])
+    starts = []
     for side in range(2):
         loads[3 + side].wait()
-        matrix = stats[side] + outer(grad, side)
-        start = matrix * (1.0 / jnp.sqrt(jnp.full((1, 1), jnp.sum(matrix * matrix), F32)))
-        scaled[side] = start
-        result[side] = jnp.where(row == column, 1.25, 0.0) - 0.25 * start
+        start = []
+        for part, lines, columns in zip(
+            parts_of(stats, side), (slice(0, middle), slice(None)), (slice(0, middle), slice(middle, None))
+        ):
+            if side == 0:
+                pair, dims = (grad[lines], grad[columns]), (((1,), (1,)), ((), ()))
+            else:
+                pair, dims = (grad[:, lines], grad[:, columns]), (((0,), (0,)), ((), ()))
+            start.append(part + lax.dot_general(*pair, dims, preferred_element_type=F32))
+        starts.append(start)
+    for side in range(2):
+        corner, right_half = starts[side]
+        squares = jnp.sum(corner * corner) + jnp.sum(right_half * right_half)
+        squares = squares + jnp.sum(right_half[:middle] * right_half[:middle])
+        inverse = 1.0 / jnp.sqrt(jnp.full((1, 1), squares, F32))
+        value = (corner * inverse, right_half * inverse)
+        put_parts(scaled, side, value)
+        put_operand(scaled_operand, side, value)
+        root = combine(identity, 1.0, value, -0.25)
+        put_parts(result, side, root)
+        put_operand(result_operand, side, root)
 
     @pl.loop(1, ITERS)
     def _(iteration):
+        excess = []
         for side in range(2):
-            value = scaled[side]
-            excess = product(value, value) * 0.0625 - 0.625 * value
-            change = product(excess, excess) + 3.125 * excess
-            value = product(change, value) + 2.44140625 * value
-            scaled[side] = value
-            root = result[side]
-            result[side] = 1.25 * root - 0.25 * product(root, value)
+            square = symmetric_product(scaled_operand, scaled_operand, side)
+            excess.append(combine(square, 0.0625, parts_of(scaled, side), -0.625))
+            put_operand(excess_operand, side, excess[side])
+        for side in range(2):
+            change = symmetric_product(excess_operand, excess_operand, side)
+            put_operand(change_operand, side, combine(change, 1.0, excess[side], 3.125))
+        for side in range(2):
+            value = symmetric_product(change_operand, scaled_operand, side)
+            value = combine(value, 1.0, parts_of(scaled, side), 2.44140625)
+            put_parts(scaled, side, value)
+            put_operand(scaled_operand, side, value)
+        for side in range(2):
+            root = symmetric_product(result_operand, scaled_operand, side)
+            root = combine(root, -0.25, parts_of(result, side), 1.25)
+            put_parts(result, side, root)
+            put_operand(result_operand, side, root)
 
         @pl.when(iteration == 3)
         def _():
@@ -480,7 +546,7 @@
             keep_vocab.wait()
             vocab_ring.start()
 
-    shampoo = product(product(result[0], grad), result[1])
+    shampoo = product(product(result_operand[0], grad).astype(BF16), result_operand[1])
     for copy, arrival in total_copies:
         arrival.wait_recv()
     entries = float(order * order)
@@ -563,6 +629,10 @@
             pltpu.VMEM((2, order, order), F32),
             pltpu.VMEM((2, order, order), F32),
             pltpu.VMEM((2, order, order), F32),
+            pltpu.VMEM((2, order, order), BF16),
+            pltpu.VMEM((2, order, order), BF16),
+            pltpu.VMEM((2, order, order), BF16),
+            pltpu.VMEM((2, order, order), BF16),
             pltpu.VMEM(row_shape[1:], BF16),
             dma((11,)),
             dma((6,)),

time: 77.9 us -> 74.2 us (0.953)
  Pallas kernels: 77 us -> 73.4 us
    pallas_call x1, Pallas kernels: 73.2 us -> 69.6 us  [shampoo_step(): pl.pallas_call(functools.partial(step_kernel, shards), out_shape=(jax.Sha...]
where the time goes in v5:
time: 74.2 us
  Pallas kernels  73.4 us (99%)
    pallas_call x1, Pallas kernels, shampoo_step(): pl.pallas_call(functools.partial(step_kernel, shards), out_shape=(jax.Sha...  69.6 us
    pallas_call x1, Pallas kernels, finish(): pl.pallas_call(finish_kernel, out_shape=(jax.ShapeDtypeStruct(direction,...  3.82 us

profile of v5, /device:TPU:8, one launch (start us, length us, event | category | flops | bytes accessed | tf_op | source)
XLA Modules:
  0.0 74.2 jit_solution(8798675322868503641)
XLA Ops:
  0.6 0.0 copy-start
  0.6 0.0 copy-start.1
  0.7 0.0 copy-start.2
  0.7 0.0 copy-start.3
  0.7 0.0 copy-start.4
  0.7 69.6 %shampoo_step.1 = (bf16[2,4,64,8,128]{4,3,2,1,0:T(8,128)(2,1)S(1)}, bf16[4,64,8,128]{3,2,1,0:T(8,128)(2,1)S(1)}, bf16[4,2,8,2048]{3,2,1,0:T(8,128)(2,1)S(1)}, bf16[4,64,8,256]{3,2,1,0:T(8,128)(2,1)S(1)}) custom-call(s32[1,64]{1,0:T(1,128)} %bitcast.3, bf16[64,8,512]{2,1,0:T(8,128)(2,1)} %bitcast.4, f32[64,8,512]{2,1,0:T(8,128)} %accum_ref.3, ...), custom_call_target="tpu_custom_call" | custom-call | tf_op jit(solution)/shard_map/shampoo_step/pallas_call | solution.py:603
  70.3 0.0 copy-done
  70.3 0.0 copy-done.1
  70.3 0.0 copy-done.2
  70.3 0.0 copy-done.3
  70.3 0.0 copy-done.4
  70.3 3.8 %finish.1 = (bf16[64,8,512]{2,1,0:T(8,128)(2,1)}, f32[64,8,512]{2,1,0:T(8,128)}, f32[2,512,512]{2,1,0:T(8,128)}, f32[2,512,512]{2,1,0:T(8,128)}, f32[2,8,8192]{2,1,0:T(8,128)}, /*index=5*/bf16[2,8,8192]{2,1,0:T(8,128)(2,1)}) custom-call(s32[64]{0:T(128)S(1)} %copy-done.4, bf16[2,4,64,8,128]{4,3,2,1,0:T(8,128)(2,1)S(1)} %get-tuple-element.10.slots_ref, ...), custom_call_target="tpu_custom_call" | custom-call | tf_op jit(solution)/shard_map/finish/pallas_call | solution.py:733
Async XLA Ops:
  0.6 69.7 %copy-start = (f32[2,512,512]{2,1,0:T(8,128)S(1)}, f32[2,512,512]{2,1,0:T(8,128)}, u32[]{:S(2)}) copy-start(f32[2,512,512]{2,1,0:T(8,128)} %left_ref.3) | copy-start | bytes 6291460
  0.6 69.7 %copy-start.1 = (f32[2,512,512]{2,1,0:T(8,128)S(1)}, f32[2,512,512]{2,1,0:T(8,128)}, u32[]{:S(2)}) copy-start(f32[2,512,512]{2,1,0:T(8,128)} %right_ref.3) | copy-start | bytes 6291460
  0.7 69.7 %copy-start.2 = (f32[64,8,512]{2,1,0:T(8,128)S(1)}, f32[64,8,512]{2,1,0:T(8,128)}, u32[]{:S(2)}) copy-start(f32[64,8,512]{2,1,0:T(8,128)} %accum_ref.3) | copy-start | bytes 3145732
  0.7 69.7 %copy-start.3 = (f32[2,8,8192]{2,1,0:T(8,128)S(1)}, f32[2,8,8192]{2,1,0:T(8,128)}, u32[]{:S(2)}) copy-start(f32[2,8,8192]{2,1,0:T(8,128)} %vocab_accum_ref.1) | copy-start | bytes 1572868
  0.7 69.7 %copy-start.4 = (s32[64]{0:T(128)S(1)}, s32[64]{0:T(128)}, u32[]{:S(2)}) copy-start(s32[64]{0:T(128)} %slot_ref.1) | copy-start | bytes 772

commit v6 on v5

--- a/solution.py
+++ b/solution.py
@@ -9,8 +9,8 @@
 
 ITERS = 6
 REP = 4
-GROUPS = 4
-TURNS = (0, 1, 3, 2)
+GROUPS = 2
+TURNS = (0, 1)
 MESH = pl.DeviceIdType.MESH
 F32 = jnp.float32
 BF16 = jnp.bfloat16
@@ -35,7 +35,7 @@
     barrier = pltpu.get_barrier_semaphore()
 
     size = shards // GROUPS
-    for turn in (2, 1, 3, 0):
+    for turn in reversed(TURNS):
         group = lax.rem(own // size + turn, GROUPS)
 
         @pl.loop(1 if turn == 0 else 0, size)
@@ -278,10 +278,18 @@
     vocab_ref,
     left_ref,
     right_ref,
-    slots_out,
-    grad_out,
+    vocab_accum_ref,
+    accum_out,
+    left_out,
+    right_out,
     vocab_out,
+    step_out,
     rows_out,
+    grad_all,
+    vocab_all,
+    accum_all,
+    vocab_accum,
+    vocab_step,
     slot_own,
     grad_own,
     grad_terms,
@@ -323,6 +331,7 @@
     sum_ring_sends,
     sum_ring_recvs,
     slot_rest_sems,
+    store_sems,
 ):
     rep, own = lax.axis_index("rep"), lax.axis_index("fsdp")
     right, left, far = (lax.rem(rep + step, REP) for step in (1, REP - 1, 2))
@@ -342,8 +351,10 @@
         pltpu.make_async_copy(grad_ref.at[:, :, grad_columns(rep)], grad_own, local_sems.at[0]),
         pltpu.make_async_copy(accum_ref.at[:, :, grad_columns(rep)], accum_own, local_sems.at[1]),
         pltpu.make_async_copy(vocab_ref.at[:, :, vocab_columns(rep)], vocab_own, local_sems.at[2]),
-        pltpu.make_async_copy(left_ref.at[pick], stats.at[0], local_sems.at[3]),
-        pltpu.make_async_copy(right_ref.at[pick], stats.at[1], local_sems.at[4]),
+        pltpu.make_async_copy(left_ref, stats.at[0], local_sems.at[3]),
+        pltpu.make_async_copy(right_ref, stats.at[1], local_sems.at[4]),
+        pltpu.make_async_copy(accum_ref, accum_all, local_sems.at[7]),
+        pltpu.make_async_copy(vocab_accum_ref, vocab_accum, local_sems.at[11]),
     )
     load_slot = pltpu.make_async_copy(slot_ref, slot_own, local_sems.at[10])
     load_slot.start()
@@ -425,7 +436,7 @@
     for copy in vocab_copies:
         copy.start()
     grad_sum[...] = total.astype(BF16)
-    keep_sum = pltpu.make_async_copy(grad_sum, grad_out.at[rep], local_sems.at[6])
+    keep_sum = pltpu.make_async_copy(grad_sum, grad_all.at[rep], local_sems.at[6])
     keep_sum.start()
 
     loads[1].wait()
@@ -458,11 +469,11 @@
     slot_rest = PairGather(slots, 0, shards, rep, own, slot_rest_sems.at[0], slot_rest_sems.at[1])
     slot_rest.start_rest()
     keep_sum.wait()
-    grad_ring = RingGather(grad_out, 0, blocks, rep, own, sum_ring_sends.at[0], sum_ring_recvs.at[0])
+    grad_ring = RingGather(grad_all, 0, blocks, rep, own, sum_ring_sends.at[0], sum_ring_recvs.at[0])
     grad_ring.start()
-    keep_vocab = pltpu.make_async_copy(vocab_sum, vocab_out.at[rep], local_sems.at[8])
+    keep_vocab = pltpu.make_async_copy(vocab_sum, vocab_all.at[rep], local_sems.at[8])
     vocab_ring = RingGather(
-        vocab_out, 0, vocab_own.shape[0], rep, own, sum_ring_sends.at[1], sum_ring_recvs.at[1]
+        vocab_all, 0, vocab_own.shape[0], rep, own, sum_ring_sends.at[1], sum_ring_recvs.at[1]
     )
     total_copies = []
     for step in range(1, REP):
@@ -484,7 +495,7 @@
         loads[3 + side].wait()
         start = []
         for part, lines, columns in zip(
-            parts_of(stats, side), (slice(0, middle), slice(None)), (slice(0, middle), slice(middle, None))
+            (stats[side, pick, :middle, :middle], stats[side, pick, :, middle:]), (slice(0, middle), slice(None)), (slice(0, middle), slice(middle, None))
         ):
             if side == 0:
                 pair, dims = (grad[lines], grad[columns]), (((1,), (1,)), ((), ()))
@@ -574,13 +585,38 @@
     grad_ring.forward()
     vocab_ring.forward()
     slot_rest.finish_rest()
-    keep_slots = pltpu.make_async_copy(slots, slots_out, local_sems.at[7])
-    keep_slots.start()
-    rows_sent = gather_groups(RingGather, row_exchange, rows_out, keep_rows, row_ring_sends, row_ring_recvs)
-
+
+    stores = []
+
+    def store(source, target):
+        stores.append(pltpu.make_async_copy(source, target, store_sems.at[len(stores)]))
+        stores[-1].start()
+
+    for slot in range(2):
+        grad = gradient(slots, slot)
+        for side, out in enumerate((left_out, right_out)):
+            stats[side, slot] = stats[side, slot] + outer(grad, side)
+            store(stats.at[side, slot], out.at[slot])
+    loads[5].wait()
+    loads[6].wait()
     grad_ring.finish()
     vocab_ring.finish()
-    keep_slots.wait()
+    for index in range(REP):
+        columns = slice(index * quarter, (index + 1) * quarter)
+        grad = grad_all[index].astype(F32)
+        accum_all[:, :, columns] = accum_all[:, :, columns] + grad * grad
+        columns = slice(index * vocab_quarter, (index + 1) * vocab_quarter)
+        vocab = vocab_all[index].astype(F32)
+        value = vocab_accum[:, :, columns] + vocab * vocab
+        vocab_accum[:, :, columns] = value
+        vocab_step[:, :, columns] = (vocab / (jnp.sqrt(value) + 1e-10)).astype(BF16)
+    store(accum_all, accum_out)
+    store(vocab_accum, vocab_out)
+    store(vocab_step, step_out)
+    rows_sent = gather_groups(RingGather, row_exchange, rows_out, keep_rows, row_ring_sends, row_ring_recvs)
+
+    for copy in stores:
+        copy.wait()
     for copy in grad_copies + vocab_copies:
         copy.wait_send()
     for copy, arrival in total_copies:
@@ -592,7 +628,7 @@
     rows_sent()
 
 
-def shampoo_step(block_slot, grads, accum, vocab, left, right):
+def shampoo_step(block_slot, grads, accum, vocab, left, right, vocab_accum):
     shards = lax.axis_size("fsdp")
     blocks, rows, order = grads.shape
     quarter = order // REP
@@ -603,14 +639,21 @@
     return pl.pallas_call(
         functools.partial(step_kernel, shards),
         out_shape=(
-            jax.ShapeDtypeStruct(slot_shape, BF16),
-            jax.ShapeDtypeStruct((REP, blocks, rows, quarter), BF16),
-            jax.ShapeDtypeStruct((REP,) + vocab_shape, BF16),
+            jax.ShapeDtypeStruct(accum.shape, F32),
+            jax.ShapeDtypeStruct(left.shape, F32),
+            jax.ShapeDtypeStruct(right.shape, F32),
+            jax.ShapeDtypeStruct(vocab_accum.shape, F32),
+            jax.ShapeDtypeStruct(vocab_accum.shape, BF16),
             jax.ShapeDtypeStruct(row_shape, BF16),
         ),
-        in_specs=[HBM] * 6,
-        out_specs=(ANY, ANY, ANY, ANY),
+        in_specs=[HBM] * 7,
+        out_specs=(ANY,) * 6,
         scratch_shapes=[
+            pltpu.VMEM((REP, blocks, rows, quarter), BF16),
+            pltpu.VMEM((REP,) + vocab_shape, BF16),
+            pltpu.VMEM(accum.shape, F32),
+            pltpu.VMEM(vocab_accum.shape, F32),
+            pltpu.VMEM(vocab_accum.shape, BF16),
             pltpu.VMEM((1, blocks), jnp.int32),
             pltpu.VMEM((blocks, rows, quarter), BF16),
             pltpu.VMEM((REP - 1, blocks, rows, quarter), BF16),
@@ -626,7 +669,7 @@
             pltpu.VMEM((1, 2 * shards), F32),
             pltpu.VMEM((shards, 1, 2 * shards), F32),
             pltpu.VMEM((REP, 1, 2 * shards), F32),
-            pltpu.VMEM((2, order, order), F32),
+            pltpu.VMEM((2, 2, order, order), F32),
             pltpu.VMEM((2, order, order), F32),
             pltpu.VMEM((2, order, order), F32),
             pltpu.VMEM((2, order, order), BF16),
@@ -634,7 +677,7 @@
             pltpu.VMEM((2, order, order), BF16),
             pltpu.VMEM((2, order, order), BF16),
             pltpu.VMEM(row_shape[1:], BF16),
-            dma((11,)),
+            dma((12,)),
             dma((6,)),
             dma((6,)),
             dma((2 * (REP - 1),)),
@@ -652,6 +695,7 @@
             dma((2, 4)),
             dma((2, 4)),
             dma((2, 6)),
+            dma((7,)),
         ],
         compiler_params=pltpu.CompilerParams(
             collective_id=0, has_side_effects=True, vmem_limit_bytes=30 * 1024 * 1024
@@ -660,61 +704,21 @@
     )(
         *(
             pltpu.with_memory_space_constraint(array, pltpu.HBM)
-            for array in (block_slot.reshape(1, -1), grads, accum, vocab, left, right)
-        )
-    )
-
-
-def finish_kernel(
-    slot_ref,
-    slots_ref,
-    grad_ref,
-    vocab_ref,
-    rows_ref,
-    accum_ref,
-    left_ref,
-    right_ref,
-    vocab_accum_ref,
-    direction_out,
-    accum_out,
-    left_out,
-    right_out,
-    vocab_out,
-    step_out,
-    direction,
-    accum,
-    stats,
-    vocab_accum,
-    vocab_step,
-    sems,
-):
+            for array in (block_slot.reshape(1, -1), grads, accum, vocab, left, right, vocab_accum)
+        )
+    )
+
+
+def finish_kernel(slot_ref, rows_ref, *refs):
+    count = (len(refs) - 2) // 2
+    sources, (direction_out, *targets), (direction, sems) = refs[:count], refs[count:-2], refs[-2:]
+    stores = [
+        pltpu.make_async_copy(source, target, sems.at[index])
+        for index, (source, target) in enumerate(zip(sources, targets))
+    ]
+    for copy in stores:
+        copy.start()
     half = rows_ref.shape[-1]
-    stores = []
-
-    def store(source, target):
-        stores.append(pltpu.make_async_copy(source, target, sems.at[len(stores)]))
-        stores[-1].start()
-
-    for slot in range(2):
-        grad = gradient(slots_ref, slot)
-        for side, (ref, out) in enumerate(((left_ref, left_out), (right_ref, right_out))):
-            stats[side, slot] = ref[slot] + outer(grad, side)
-            store(stats.at[side, slot], out.at[slot])
-    for index in range(REP):
-        quarter = grad_ref.shape[-1]
-        columns = slice(index * quarter, (index + 1) * quarter)
-        grad = grad_ref[index].astype(F32)
-        accum[:, :, columns] = accum_ref[:, :, columns] + grad * grad
-    store(accum, accum_out)
-    for index in range(REP):
-        quarter = vocab_ref.shape[-1]
-        columns = slice(index * quarter, (index + 1) * quarter)
-        vocab = vocab_ref[index].astype(F32)
-        value = vocab_accum_ref[:, :, columns] + vocab * vocab
-        vocab_accum[:, :, columns] = value
-        vocab_step[:, :, columns] = (vocab / (jnp.sqrt(value) + 1e-10)).astype(BF16)
-    store(vocab_accum, vocab_out)
-    store(vocab_step, step_out)
 
     @pl.loop(0, direction.shape[0], unroll=4)
     def _(block):
@@ -723,47 +727,33 @@
         for side in range(2):
             direction[block, :, side * half : (side + 1) * half] = rows_ref[2 * pick + side, owner]
 
-    store(direction, direction_out)
+    stores.append(pltpu.make_async_copy(direction, direction_out, sems.at[count]))
+    stores[-1].start()
     for copy in stores:
         copy.wait()
 
 
-def finish(block_slot, slots, grads, vocab, rows, accum, left, right, vocab_accum):
+def finish(block_slot, rows, *others):
     direction = (block_slot.shape[0], rows.shape[2], 2 * rows.shape[3])
     return pl.pallas_call(
         finish_kernel,
-        out_shape=(
-            jax.ShapeDtypeStruct(direction, BF16),
-            jax.ShapeDtypeStruct(accum.shape, F32),
-            jax.ShapeDtypeStruct(left.shape, F32),
-            jax.ShapeDtypeStruct(right.shape, F32),
-            jax.ShapeDtypeStruct(vocab_accum.shape, F32),
-            jax.ShapeDtypeStruct(vocab_accum.shape, BF16),
-        ),
-        in_specs=[SMEM] + [VMEM] * 8,
-        out_specs=(HBM,) * 6,
-        scratch_shapes=[
-            pltpu.VMEM(direction, BF16),
-            pltpu.VMEM(accum.shape, F32),
-            pltpu.VMEM((2,) + left.shape, F32),
-            pltpu.VMEM(vocab_accum.shape, F32),
-            pltpu.VMEM(vocab_accum.shape, BF16),
-            pltpu.SemaphoreType.DMA((8,)),
-        ],
-        compiler_params=pltpu.CompilerParams(vmem_limit_bytes=30 * 1024 * 1024),
+        out_shape=(jax.ShapeDtypeStruct(direction, BF16),)
+        + tuple(jax.ShapeDtypeStruct(other.shape, other.dtype) for other in others),
+        in_specs=[SMEM, VMEM] + [ANY] * len(others),
+        out_specs=(HBM,) * (1 + len(others)),
+        scratch_shapes=[pltpu.VMEM(direction, BF16), pltpu.SemaphoreType.DMA((1 + len(others),))],
+        compiler_params=pltpu.CompilerParams(vmem_limit_bytes=8 * 1024 * 1024),
         name="finish",
-    )(block_slot, slots, grads, vocab, rows, accum, left, right, vocab_accum)
+    )(block_slot, rows, *others)
 
 
 def on_device(
     grad_blocks, graft_accum, left_stats, right_stats, block_slot, vocab_grads, vocab_accum
 ):
-    slots, grads, vocab, rows = shampoo_step(
-        block_slot, grad_blocks[0], graft_accum, vocab_grads[0], left_stats, right_stats
-    )
-    return finish(
-        block_slot, slots, grads, vocab, rows, graft_accum, left_stats, right_stats, vocab_accum
-    )
+    *others, rows = shampoo_step(
+        block_slot, grad_blocks[0], graft_accum, vocab_grads[0], left_stats, right_stats, vocab_accum
+    )
+    return tuple(finish(block_slot, rows, *others))
 
 
 def solution(mesh):

time: 74.2 us -> 73.4 us (0.989); the launches traced: 74.2 us -> 72.2 us
  Pallas kernels: 73.4 us -> 71.5 us
    pallas_call x1, Pallas kernels: 69.6 us -> 68.1 us  [shampoo_step(): pl.pallas_call(functools.partial(step_kernel, shards), out_shape=(jax.Sha...]
where the time goes in v6:
time: 73.4 us; the launch traced here: 72.2 us
  Pallas kernels  71.5 us (97%)
    pallas_call x1, Pallas kernels, shampoo_step(): pl.pallas_call(functools.partial(step_kernel, shards), out_shape=(jax.Sha...  68.1 us
    pallas_call x1, Pallas kernels, finish(): pl.pallas_call(finish_kernel, out_shape=(jax.ShapeDtypeStruct(direction,...  3.35 us

profile of v6, /device:TPU:8, one launch (start us, length us, event | category | flops | bytes accessed | tf_op | source)
XLA Modules:
  0.0 72.2 jit_solution(15007827169676004540)
XLA Ops:
  0.6 0.0 copy-start
  0.6 68.1 %shampoo_step.1 = (f32[64,8,512]{2,1,0:T(8,128)S(1)}, f32[2,512,512]{2,1,0:T(8,128)S(1)}, f32[2,512,512]{2,1,0:T(8,128)S(1)}, f32[2,8,8192]{2,1,0:T(8,128)S(1)},...) custom-call(s32[1,64]{1,0:T(1,128)} %bitcast.3, bf16[64,8,512]{2,1,0:T(8,128)(2,1)} %bitcast.4, ...), custom_call_target="tpu_custom_call" | custom-call | tf_op jit(solution)/shard_map/shampoo_step/pallas_call | solution.py:639
  68.8 0.0 copy-done
  68.8 3.3 %finish.1 = (bf16[64,8,512]{2,1,0:T(8,128)(2,1)}, f32[64,8,512]{2,1,0:T(8,128)}, f32[2,512,512]{2,1,0:T(8,128)}, f32[2,512,512]{2,1,0:T(8,128)}, f32[2,8,8192]{2,1,0:T(8,128)}, /*index=5*/bf16[2,8,8192]{2,1,0:T(8,128)(2,1)}) custom-call(s32[64]{0:T(128)S(1)} %copy-done, bf16[4,64,8,256]{3,2,1,0:T(8,128)(2,1)S(1)} %get-tuple-element.12.rows_ref, ...), custom_call_target="tpu_custom_call" | custom-call | tf_op jit(solution)/shard_map/finish/pallas_call | solution.py:738
Async XLA Ops:
  0.6 68.2 %copy-start = (s32[64]{0:T(128)S(1)}, s32[64]{0:T(128)}, u32[]{:S(2)}) copy-start(s32[64]{0:T(128)} %slot_ref.1) | copy-start | bytes 772
